TPU v7x, 256 devices: a whole 4x4x8 slice. The times are simulated.
256 devices in a mesh: row: 32 (over y, z_lo, core), col: 8 (over x, z_hi).
Axes of the slice: x: 4, y: 4, z: 8 (z_hi: 2, z_lo: 4; z = z_hi * 4 + z_lo), core: 2. Of those that a mesh axis runs over, the one named last changes fastest.
Arguments:
- frames: bfloat16 [256, 3, 12288], P('col', None, 'row'), may hold values from -6 to 6
- rotations: float32 [3, 3, 256], replicated, may hold values from -1 to 1, as said below
- inverse_cov: float32 [12288, 12288], P('row', 'col'), may hold values from -1 to 11, as said below
Outputs:
- covariance: float32 [12288, 12288], P('row', 'col')
- fitted_rotations: float32 [3, 3, 256], P(None, None, 'col')
Inputs may be any that keep to these rules, and one draw needn't show every extreme that they name: `rotations`: each frame's 3 x 3 matrix is a rotation. `inverse_cov`: symmetric.
All inputs are finite; a program needn't handle non-finite values.
Results may differ from a plain program's by a relative error of at most 0.00031.
Values may be sent and summed in bfloat16 or wider, within the bound.
A program may use at most 64 MiB of HBM per device.

v0:
```python
import jax
import jax.numpy as jnp
from jax import lax
from jax.sharding import PartitionSpec as P

POLAR = 12


def orthogonalize(fitted):
    scaling = jnp.sqrt(1.0 + jnp.sum(fitted * fitted, axis=(0, 1)))
    current = jnp.transpose(fitted, (1, 0, 2)) / scaling
    for sweep in range(POLAR):
        square = jnp.einsum("ijf,kjf->ikf", current, current, precision=lax.Precision.HIGHEST)
        cubed_term = jnp.einsum("ikf,klf->ilf", square, current, precision=lax.Precision.HIGHEST)
        current = 1.5 * current - 0.5 * cubed_term
    return current


def deviations_of(transforms, coords_half, centre_block):
    moved = jnp.einsum(
        "klf,fla->fka", transforms, coords_half.astype(jnp.float32), precision=lax.Precision.HIGHEST
    )
    values = (moved - centre_block[None]).astype(jnp.bfloat16)
    return values.reshape(values.shape[0] * 3, values.shape[2])


def tile_block(rows_operand, column_panel):
    return lax.dot_general(
        rows_operand, column_panel, (((0,), (0,)), ((), ())), preferred_element_type=jnp.float32
    )


def per_device(frames, rotations, inverse_cov):
    col_width = inverse_cov.shape[1]
    col_count = lax.axis_size("col")
    col_index = lax.axis_index("col")
    frame_total = frames.shape[0] * col_count
    offset = col_index * frames.shape[0]
    local_rot = lax.dynamic_slice_in_dim(rotations, offset, frames.shape[0], 2)
    coords = frames.astype(jnp.float32)
    partial_value = jnp.einsum("klf,fla->ka", local_rot, coords, precision=lax.Precision.HIGHEST)
    centre_rows = lax.psum(partial_value, "col") / frame_total
    centre_all = lax.all_gather(centre_rows, "row", axis=1, tiled=True)
    centre_cols = lax.dynamic_slice_in_dim(centre_all, col_index * col_width, col_width, 1)
    local_weight = lax.dot_general(
        centre_cols, inverse_cov, (((1,), (1,)), ((), ())), precision=lax.Precision.HIGHEST
    )
    weighted = lax.psum(local_weight, "col")
    fit_part = jnp.einsum("fka,la->klf", coords, weighted, precision=lax.Precision.HIGHEST)
    fitted = lax.psum(fit_part, "row")
    transforms = orthogonalize(fitted)
    local_dev = deviations_of(transforms, frames, centre_rows)
    rows_operand = lax.all_gather(local_dev, "col", axis=0, tiled=True)
    dev_atoms = lax.all_gather(local_dev, "row", axis=1, tiled=True)
    column_panel = lax.all_to_all(dev_atoms, "col", split_axis=1, concat_axis=0, tiled=True)
    covariance = tile_block(rows_operand, column_panel) / (3 * frame_total)
    return (covariance, transforms)


def solution(mesh):
    placed = (P("col", None, "row"), P(), P("row", "col"))
    return jax.shard_map(
        per_device,
        mesh=mesh,
        in_specs=placed,
        out_specs=(P("row", "col"), P(None, None, "col")),
        check_vma=False,
    )
```

profile of v0, /device:TPU:40, one launch (start us, length us, event | category | flops | bytes accessed | tf_op | source)
XLA Modules:
  0.0 377.9 jit_solution(10751000671556221047)
XLA Ops:
  7.2 0.9 constant_dynamic-slice_fusion
  8.2 1.1 convolution_bitcast_fusion.13
  9.3 32.8 %psum.21 = f32[3,384]{1,0:T(4,128)S(1)} all-reduce(f32[3,384]{1,0:T(4,128)S(1)} %convolution_bitcast_fusion.13), channel_id=1, replica_groups=mesh['row'=32,'col'=8] {'col'}, use_global_device_ids=true, to_apply=%region_0.0 | all-reduce | flops 1152 | bytes 9216 | tf_op jit(solution)/shard_map/psum | solution.py:42
  42.1 34.4 %all_gather.9 = f32[3,12288]{1,0:T(4,128)S(1)} all-gather(f32[3,384]{1,0:T(4,128)S(1)} %broadcast_multiply_fusion), channel_id=1, replica_groups=mesh['row'=32,'col'=8] {'row'}, dimensions={1}, use_global_device_ids=true | all-gather | bytes 152064 | tf_op jit(solution)/shard_map/all_gather | solution.py:43
  76.5 2.0 fusion.2
  78.5 24.2 %psum.22 = f32[3,384]{1,0:T(4,128)S(1)} all-reduce(f32[3,384]{1,0:T(4,128)S(1)} %fusion.2), channel_id=1, replica_groups=mesh['row'=32,'col'=8] {'col'}, use_global_device_ids=true, to_apply=%region_1.0 | all-reduce | flops 1152 | bytes 9216 | tf_op jit(solution)/shard_map/psum | solution.py:48
  102.9 56.1 %psum.23 = f32[3,3,32]{2,1,0:T(4,128)S(1)} all-reduce(f32[3,3,32]{2,1,0:T(4,128)S(1)} %convolution_bitcast_fusion.12), channel_id=1, replica_groups=mesh['row'=32,'col'=8] {'row'}, use_global_device_ids=true, to_apply=%region_2.0 | all-reduce | flops 288 | bytes 2304 | tf_op jit(solution)/shard_map/psum | solution.py:50
  159.2 0.4 convolution_bitcast_fusion.11
  160.2 0.4 convolution_bitcast_fusion.10
  161.2 0.4 convolution_bitcast_fusion.9
  162.2 0.4 convolution_bitcast_fusion.8
  163.2 0.4 convolution_bitcast_fusion.7
  164.2 0.4 convolution_bitcast_fusion.6
  165.2 0.4 convolution_bitcast_fusion.5
  166.2 0.4 convolution_bitcast_fusion.4
  167.2 0.4 convolution_bitcast_fusion.3
  168.3 0.4 convolution_bitcast_fusion.2
  171.6 0.7 reshape.15
  172.4 77.7 %all-gather.2.cloned.1.call-done = bf16[96,12288]{1,0:T(8,128)(2,1)} async-done(((bf16[96,384]{1,0:T(8,128)(2,1)}), bf16[96,12288]{1,0:T(8,128)(2,1)}) %all-gather.2.cloned.1.call-update) | async-done | bytes 2359312 | tf_op jit(solution)/shard_map/all_gather | solution.py:54
  250.1 3.3 copy.83
  253.4 8.1 %all-to-all-start = ((bf16[96,8,1536]{2,0,1:T(8,128)(2,1)}), bf16[96,8,1536]{2,0,1:T(8,128)(2,1)}, u32[]{:S(2)}, u32[]{:S(2)}) async-start(bf16[96,8,1536]{2,0,1:T(8,128)(2,1)} %bitcast.118), calls=%async_computation | async-start | bytes 4718592 | tf_op jit(solution)/shard_map/all_to_all | solution.py:55
  261.5 0.6 copy.63
  262.1 104.9 %all_gather.10 = bf16[768,384]{1,0:T(8,128)(2,1)S(1)} all-gather(bf16[96,384]{1,0:T(8,128)(2,1)S(1)} %copy-done.1), channel_id=1, replica_groups=mesh['row'=32,'col'=8] {'col'}, dimensions={0}, use_global_device_ids=true | all-gather | bytes 663552 | tf_op jit(solution)/shard_map/all_gather | solution.py:53
  366.9 4.2 %convolution_multiply_fusion = f32[384,1536]{1,0:T(8,128)} fusion(bf16[768,384]{1,0:T(8,128)(2,1)S(1)} %all_gather.10, bf16[768,1536]{1,0:T(8,128)(2,1)} %bitcast.29), kind=kOutput, calls=%fused_computation | convolution fusion | flops 906559488 | bytes 5308416 | tf_op jit(solution)/shard_map/dot_general | solution.py:28
  (66 shorter events, 8.4 us)
Async XLA Ops:
  7.2 69.3 %copy-start = (f32[384,1536]{1,0:T(8,128)S(1)}, f32[384,1536]{1,0:T(8,128)}, u32[]{:S(2)}) copy-start(f32[384,1536]{1,0:T(8,128)} %param.5) | copy-start | bytes 7077892
  7.2 95.5 %copy-start.2 = (bf16[32,3,384]{2,0,1:T(8,128)(2,1)S(1)}, bf16[32,3,384]{2,0,1:T(8,128)(2,1)}, u32[]{:S(2)}) copy-start(bf16[32,3,384]{2,0,1:T(8,128)(2,1)} %param.3) | copy-start | bytes 221188
  7.2 242.9 %all-gather.2.cloned.1.call-start = ((), (), s32[]{:S(2)}) async-start(), calls=%async_computation.1 | async-start | bytes 2433024 | tf_op jit(solution)/shard_map/all_gather | solution.py:54
  253.4 8.7 %copy-start.1 = (bf16[96,384]{1,0:T(8,128)(2,1)S(1)}, bf16[96,384]{1,0:T(8,128)(2,1)}, u32[]{:S(2)}) copy-start(bf16[96,384]{1,0:T(8,128)(2,1)} %reshape.15) | copy-start | bytes 221188
  253.4 113.6 %all-to-all-start = ((bf16[96,8,1536]{2,0,1:T(8,128)(2,1)}), bf16[96,8,1536]{2,0,1:T(8,128)(2,1)}, u32[]{:S(2)}, u32[]{:S(2)}) async-start(bf16[96,8,1536]{2,0,1:T(8,128)(2,1)} %bitcast.118), calls=%async_computation | async-start | bytes 4718592 | tf_op jit(solution)/shard_map/all_to_all | solution.py:55
Sparse Core Ops, SparseCore 0:
  172.5 77.5 all-gather.1
where the time goes:
time: 378 us
  blocking collectives  252 us (67%)
  waiting for transfers between devices  77.7 us (21%)
  matrix products  17.1 us (5%)
  between operations  14.4 us (4%)
  starting transfers between devices  8.13 us (2%)
  local copies, waits for them, and re-layouts  8.1 us (2%)
    all_gather x1, blocking collectives, per_device(): rows_operand = lax.all_gather(local_dev, 'col', axis=0, tiled=True)  105 us
    all_gather x1, waiting for transfers between devices, per_device(): dev_atoms = lax.all_gather(local_dev, 'row', axis=1, tiled=True)  77.7 us
    psum x1, blocking collectives, per_device(): fitted = lax.psum(fit_part, 'row')  56.1 us
    all_gather x1, blocking collectives, per_device(): centre_all = lax.all_gather(centre_rows, 'row', axis=1, tiled=True)  34.4 us
    psum x1, blocking collectives, per_device(): centre_rows = lax.psum(partial_value, 'col') / frame_total  32.8 us
    psum x1, blocking collectives, per_device(): weighted = lax.psum(local_weight, 'col')  24.2 us
    all_to_all x1, starting transfers between devices, per_device(): lax.all_to_all(dev_atoms, 'col', split_axis=1, concat_axis=0, tiled=True)  8.09 us
  transfers between devices with their start and end apart: 2, of which 1 were waited for; matrix products, arithmetic and copies ran while one was open for 0% of the time, Pallas kernels for 0%

commit v1 on v0

v1 whole, which is shorter than its diff:
```python
import functools

import jax
import jax.numpy as jnp
from jax import lax
from jax.experimental import pallas as pl
from jax.experimental.pallas import tpu as pltpu
from jax.sharding import PartitionSpec as P

POLAR = 12
ROWS = 32
COLS = 8
FB = 32
SUB = 4
ATOMS_LOCAL = 384
FRAMES = ROWS * COLS
MESH = pl.DeviceIdType.MESH
F32 = jnp.float32
BF16 = jnp.bfloat16


def split3(value):
    high = value.astype(BF16)
    rest = value - high.astype(F32)
    middle = rest.astype(BF16)
    low = (rest - middle.astype(F32)).astype(BF16)
    return high, middle, low


def contract(left, right, dims):
    return lax.dot_general(left, right, (dims, ((), ())), preferred_element_type=F32)


def remote(src, dst, send, recv, row, col):
    return pltpu.make_async_remote_copy(
        src_ref=src, dst_ref=dst, send_sem=send, recv_sem=recv, device_id=(row, col), device_id_type=MESH
    )


def polar_all(fit):
    total = jnp.zeros_like(fit[0][0])
    for k in range(3):
        for l in range(3):
            total = total + fit[k][l] * fit[k][l]
    scaling = jnp.sqrt(1.0 + total)
    cur = [[fit[k][i] / scaling for k in range(3)] for i in range(3)]
    for _ in range(POLAR):
        square = [[None] * 3 for _ in range(3)]
        for i in range(3):
            for k in range(i, 3):
                value = cur[i][0] * cur[k][0] + cur[i][1] * cur[k][1] + cur[i][2] * cur[k][2]
                square[i][k] = value
                square[k][i] = value
        nxt = [[None] * 3 for _ in range(3)]
        for i in range(3):
            for l in range(3):
                cubed = square[i][0] * cur[0][l] + square[i][1] * cur[1][l] + square[i][2] * cur[2][l]
                nxt[i][l] = 1.5 * cur[i][l] - 0.5 * cubed
        cur = nxt
    return cur


def kernel(
    x_ref, rot_ref, w_hbm, cov_hbm, tr_ref,
    wv, cpart, cbuf, wsend, wbuf, fsend, fbuf, gsend, gbuf, rbuf, pbuf, acc, coef, wide, dev_rows, dev_q, out,
    w_sem, out_sem, c_send, c_recv, w_send, w_recv, f_send, f_recv, g_send, g_recv, r_send, r_recv, p_send, p_recv,
    s_send, s_recv,
):
    row = lax.axis_index("row")
    col = lax.axis_index("col")
    core = row % 2
    sibling = row + 1 - 2 * core
    panel_col = row // SUB
    sub = row % SUB
    is_self = panel_col == col

    w_copy = pltpu.make_async_copy(w_hbm, wv, w_sem)
    w_copy.start()

    barrier = pltpu.get_barrier_semaphore()

    def greet(r, c):
        pl.semaphore_signal(barrier, inc=1, device_id=(r, c), device_id_type=MESH)

    def greet_panel(m, carry):
        r = SUB * col + m // COLS
        c = m % COLS

        @pl.when(jnp.logical_or(r != row, c != col))
        def _():
            greet(r, c)

        return carry

    lax.fori_loop(0, 32, greet_panel, 0)
    lax.fori_loop(1, COLS, lambda m, t: (greet(row, (col + m) % COLS), t)[1], 0)
    lax.fori_loop(1, ROWS, lambda m, t: (greet((row + m) % ROWS, col), t)[1], 0)

    part = jnp.zeros((3, ATOMS_LOCAL), F32)
    for l in range(3):
        whole = rot_ref[:, l, :]
        mine = jnp.zeros((3, FB), F32)
        for i in range(COLS):
            mine = mine + jnp.where(col == i, whole[:, i * FB : (i + 1) * FB], 0.0)
        block = x_ref[l * FB : (l + 1) * FB, :]
        for piece in split3(mine):
            part = part + contract(piece, block, ((1,), (0,)))
    cpart[...] = part
    rbuf[col] = x_ref[...]

    @pl.when(is_self)
    def _():
        cbuf[sub, col] = part
        pbuf[sub, col] = x_ref[...]

    pl.semaphore_wait(barrier, 70 - is_self.astype(jnp.int32))

    def centre_copy(m):
        r = (row + m) % ROWS
        return r, remote(cpart, cbuf.at[sub, col], c_send.at[m], c_recv.at[sub, col], r, panel_col)

    def centre_start(m, carry):
        r, copy = centre_copy(m)

        @pl.when(jnp.logical_or(r != row, jnp.logical_not(is_self)))
        def _():
            copy.start()

        return carry

    lax.fori_loop(0, ROWS, centre_start, 0)

    def row_copy(m):
        c = (col + m) % COLS
        return remote(x_ref, rbuf.at[col], r_send.at[m], r_recv.at[col], row, c)

    def panel_copy(m):
        r = 2 * ((row // 2 + m) % 16) + core
        return r, remote(x_ref, pbuf.at[sub, col], p_send.at[m], p_recv.at[sub, col], r, panel_col)

    def row_start(m, carry):
        row_copy(m).start()
        return carry

    def panel_start(m, carry):
        r, copy = panel_copy(m)

        @pl.when(jnp.logical_or(r != row, jnp.logical_not(is_self)))
        def _():
            copy.start()

        return carry

    lax.fori_loop(1, COLS, row_start, 0)
    lax.fori_loop(0, 16, panel_start, 0)

    def centre_wait(m, carry):
        q = m // COLS
        c = m % COLS

        @pl.when(jnp.logical_or(SUB * col + q != row, c != col))
        def _():
            remote(cpart, cbuf.at[q, c], c_send.at[0], c_recv.at[q, c], row, col).wait_recv()

        return carry

    lax.fori_loop(0, SUB * COLS, centre_wait, 0)
    centre_cols = jnp.sum(cbuf[...], axis=1) * (1.0 / FRAMES)

    w_copy.wait()
    lanes = [[centre_cols[q][l : l + 1, :] for q in range(SUB)] for l in range(3)]

    def weigh(i, carry):
        start = pl.multiple_of(i * 32, 32)
        sums = [jnp.zeros((32, 128), F32) for _ in range(3)]
        for q in range(SUB):
            for t in range(3):
                tile = wv[pl.ds(start, 32), q * 384 + t * 128 : q * 384 + (t + 1) * 128]
                for l in range(3):
                    sums[l] = sums[l] + tile * lanes[l][q][:, t * 128 : (t + 1) * 128]
        for l in range(3):
            acc[l, pl.ds(start, 32), :] = sums[l]
        return carry

    lax.fori_loop(0, 12, weigh, 0)
    ones = jnp.ones((8, 128), BF16)
    for l in range(3):
        line = jnp.zeros((8, ATOMS_LOCAL), F32)
        for piece in split3(acc[l]):
            line = line + contract(ones, piece, ((1,), (1,)))
        wsend[l : l + 1, :] = line[0:1, :]
    wsend[3:6, :] = cpart[...]
    wbuf[col] = wsend[...]

    def weight_copy(m):
        c = (col + m) % COLS
        return remote(wsend, wbuf.at[col], w_send.at[m], w_recv.at[col], row, c)

    def weight_start(m, carry):
        weight_copy(m).start()
        return carry

    def weight_wait(m, carry):
        c = (col + m) % COLS
        remote(wsend, wbuf.at[c], w_send.at[0], w_recv.at[c], row, col).wait_recv()
        return carry

    lax.fori_loop(1, COLS, weight_start, 0)
    lax.fori_loop(1, COLS, weight_wait, 0)
    both = jnp.sum(wbuf[...], axis=0)
    centre_rows = both[3:6, :] * (1.0 / FRAMES)

    fit = jnp.zeros((3, 96), F32)
    for piece in split3(both[0:3, :]):
        fit = fit + contract(piece, x_ref[...], ((1,), (1,)))
    fsend[...] = fit
    fbuf[row] = fit

    def fit_copy(m):
        r = (row + m) % ROWS
        return remote(fsend, fbuf.at[row], f_send.at[m], f_recv.at[row], r, col)

    def fit_start(m, carry):
        fit_copy(m).start()
        return carry

    def fit_wait(m, carry):
        r = (row + m) % ROWS
        remote(fsend, fbuf.at[r], f_send.at[0], f_recv.at[r], row, col).wait_recv()
        return carry

    lax.fori_loop(1, ROWS, fit_start, 0)
    lax.fori_loop(1, ROWS, fit_wait, 0)
    fitted = jnp.sum(fbuf[...], axis=0)
    gsend[...] = fitted
    gbuf[col] = fitted

    def gather_copy(m):
        c = (col + m) % COLS
        return remote(gsend, gbuf.at[col], g_send.at[m], g_recv.at[col], row, c)

    def gather_start(m, carry):
        gather_copy(m).start()
        return carry

    def gather_wait(m, carry):
        c = (col + m) % COLS
        remote(gsend, gbuf.at[c], g_send.at[0], g_recv.at[c], row, col).wait_recv()
        return carry

    lax.fori_loop(1, COLS, gather_start, 0)

    def panel_wait(m, carry):
        q = core + 2 * (m // COLS)
        c = m % COLS

        @pl.when(jnp.logical_or(SUB * col + q != row, c != col))
        def _():
            remote(x_ref, pbuf.at[q, c], p_send.at[0], p_recv.at[q, c], row, col).wait_recv()

        return carry

    def share_copy(j):
        q = core + 2 * j
        return remote(pbuf.at[q], pbuf.at[q], s_send.at[j], s_recv.at[q], sibling, col)

    for j in range(2):
        lax.fori_loop(j * COLS, (j + 1) * COLS, panel_wait, 0)
        share_copy(j).start()

    lax.fori_loop(1, COLS, gather_wait, 0)

    rows_of = [gbuf[:, l, :] for l in range(3)]
    turned = polar_all([[rows_of[l][:, k * FB : (k + 1) * FB] for l in range(3)] for k in range(3)])
    at_col = lax.broadcasted_iota(jnp.int32, (COLS, FB), 0) == col
    for k in range(3):
        for l in range(3):
            tr_ref[k, l : l + 1, :] = jnp.sum(jnp.where(at_col, turned[k][l], 0.0), axis=0, keepdims=True)
            coef[:, 0:FB] = turned[k][l]
            upright = jnp.transpose(coef[...])
            for c in range(COLS):
                wide[3 * k + l, c] = jnp.broadcast_to(upright[0:FB, c : c + 1], (FB, 128))

    def row_wait(m, carry):
        c = (col + m) % COLS
        remote(x_ref, rbuf.at[c], r_send.at[0], r_recv.at[c], row, col).wait_recv()
        return carry

    lax.fori_loop(1, COLS, row_wait, 0)

    def deviate(source, centre):
        base = [jnp.broadcast_to(centre[k : k + 1, :], (FB, ATOMS_LOCAL)) for k in range(3)]

        def body(c, carry):
            block = source[c].astype(F32)
            xs = [block[l * FB : (l + 1) * FB, :] for l in range(3)]
            start = pl.multiple_of(c * 96, 96)
            values = []
            for k in range(3):
                terms = []
                for l in range(3):
                    factor = wide[3 * k + l, c]
                    terms.append(jnp.concatenate([factor, factor, factor], axis=1) * xs[l])
                values.append((terms[0] + terms[1]) + terms[2] - base[k])
            dev_q[pl.ds(start, 96), :] = jnp.concatenate(values, axis=0).astype(BF16)
            return carry

        lax.fori_loop(0, COLS, body, 0)

    deviate(rbuf, centre_rows)
    dev_rows[...] = jnp.transpose(dev_q[...])

    for j in range(2):
        q = 1 - core + 2 * j
        remote(pbuf.at[q], pbuf.at[q], s_send.at[0], s_recv.at[q], row, col).wait_recv()

    def out_copy(q):
        return pltpu.make_async_copy(
            out.at[q], cov_hbm.at[:, pl.ds(pl.multiple_of(q * ATOMS_LOCAL, ATOMS_LOCAL), ATOMS_LOCAL)], out_sem.at[q]
        )

    for q in range(SUB):
        deviate(pbuf.at[q], centre_cols[q])
        out[q] = contract(dev_rows[...], dev_q[...], ((1,), (0,))) * (1.0 / (3 * FRAMES))
        out_copy(q).start()

    for q in range(SUB):
        out_copy(q).wait()

    def centre_sent(m, carry):
        r, copy = centre_copy(m)

        @pl.when(jnp.logical_or(r != row, jnp.logical_not(is_self)))
        def _():
            copy.wait_send()

        return carry

    def panel_sent(m, carry):
        r, copy = panel_copy(m)

        @pl.when(jnp.logical_or(r != row, jnp.logical_not(is_self)))
        def _():
            copy.wait_send()

        return carry

    lax.fori_loop(0, ROWS, centre_sent, 0)
    lax.fori_loop(0, 16, panel_sent, 0)
    for copy_of, count in ((row_copy, COLS), (weight_copy, COLS), (fit_copy, ROWS), (gather_copy, COLS)):
        lax.fori_loop(1, count, lambda m, t, f=copy_of: (f(m).wait_send(), t)[1], 0)
    for j in range(2):
        share_copy(j).wait_send()


def per_device(frames, rotations, inverse_cov):
    x = jnp.transpose(frames, (1, 0, 2)).reshape(96, ATOMS_LOCAL)
    dma = pltpu.SemaphoreType.DMA
    vmem = pl.BlockSpec(memory_space=pltpu.VMEM)
    hbm = pl.BlockSpec(memory_space=pl.ANY)
    return pl.pallas_call(
        kernel,
        out_shape=(
            jax.ShapeDtypeStruct((ATOMS_LOCAL, SUB * ATOMS_LOCAL), F32),
            jax.ShapeDtypeStruct((3, 3, FB), F32),
        ),
        in_specs=[vmem, vmem, hbm],
        out_specs=(hbm, vmem),
        scratch_shapes=[
            pltpu.VMEM((384, 1536), F32),
            pltpu.VMEM((3, 384), F32),
            pltpu.VMEM((4, 8, 3, 384), F32),
            pltpu.VMEM((6, 384), F32),
            pltpu.VMEM((8, 6, 384), F32),
            pltpu.VMEM((3, 96), F32),
            pltpu.VMEM((32, 3, 96), F32),
            pltpu.VMEM((3, 96), F32),
            pltpu.VMEM((8, 3, 96), F32),
            pltpu.VMEM((8, 96, 384), BF16),
            pltpu.VMEM((4, 8, 96, 384), BF16),
            pltpu.VMEM((3, 384, 128), F32),
            pltpu.VMEM((8, 128), F32),
            pltpu.VMEM((9, 8, 32, 128), F32),
            pltpu.VMEM((384, 768), BF16),
            pltpu.VMEM((768, 384), BF16),
            pltpu.VMEM((4, 384, 384), F32),
            dma(()), dma((4,)),
            dma((32,)), dma((4, 8)),
            dma((8,)), dma((8,)),
            dma((32,)), dma((32,)),
            dma((8,)), dma((8,)),
            dma((8,)), dma((8,)),
            dma((16,)), dma((4, 8)),
            dma((2,)), dma((4,)),
        ],
        compiler_params=pltpu.CompilerParams(
            collective_id=0, has_side_effects=True, vmem_limit_bytes=48 * 1024 * 1024
        ),
        name="superpose",
    )(x, rotations, inverse_cov)


def solution(mesh):
    placed = (P("col", None, "row"), P(), P("row", "col"))
    return jax.shard_map(
        per_device,
        mesh=mesh,
        in_specs=placed,
        out_specs=(P("row", "col"), P(None, None, "col")),
        check_vma=False,
    )
```

time: 378 us -> 125 us (0.33)
  the two profiles are of different devices: /device:TPU:40 before, /device:TPU:1 now
where the time goes in v1:
time: 125 us
  Pallas kernels  119 us (95%)
  local copies, waits for them, and re-layouts  5.25 us (4%)
    pallas_call x1, Pallas kernels, per_device(): pl.pallas_call(kernel, out_shape=(jax.ShapeDtypeStruct((ATOMS_LOCAL, SUB...  119 us
    unnamed x8, local copies, waits for them, and re-layouts  5.25 us

profile of v1, /device:TPU:1, one launch (start us, length us, event | category | flops | bytes accessed | tf_op | source)
XLA Modules:
  0.0 124.9 jit_solution(4157747182264644239)
XLA Ops:
  0.6 0.0 copy-start
  0.6 1.7 %copy-done = f32[384,1536]{1,0:T(8,128)S(1)} copy-done((f32[384,1536]{1,0:T(8,128)S(1)}, f32[384,1536]{1,0:T(8,128)}, u32[]{:S(2)}) %copy-start) | copy-done | bytes 2359320
  2.3 0.0 copy-start.1
  2.3 0.9 copy-done.1
  3.2 0.0 copy-start.2
  3.2 0.7 copy-done.2
  3.9 119.0 %superpose.1 = (f32[384,1536]{1,0:T(8,128)S(1)}, f32[3,3,32]{2,1,0:T(4,128)S(1)}) custom-call(bf16[96,384]{1,0:T(8,128)(2,1)S(1)} %bitcast.3, f32[3,3,256]{2,1,0:T(4,128)S(1)} %copy-done.2, f32[384,1536]{1,0:T(8,128)S(1)} %copy-done), custom_call_target="tpu_custom_call" | custom-call | tf_op jit(solution)/shard_map/superpose/pallas_call | solution.py:361
  122.9 1.4 %copy.7 = f32[384,1536]{1,0:T(8,128)} copy(f32[384,1536]{1,0:T(8,128)S(1)} %get-tuple-element.4) | data formatting | bytes 4718592
  124.3 0.6 copy.8
Async XLA Ops:
  0.6 1.7 %copy-start = (f32[384,1536]{1,0:T(8,128)S(1)}, f32[384,1536]{1,0:T(8,128)}, u32[]{:S(2)}) copy-start(f32[384,1536]{1,0:T(8,128)} %w_hbm.1) | copy-start | bytes 7077892
  2.3 0.9 copy-start.1
  3.2 0.7 copy-start.2

commit v2 on v1

--- a/solution.py
+++ b/solution.py
@@ -62,9 +62,9 @@
 
 def kernel(
     x_ref, rot_ref, w_hbm, cov_hbm, tr_ref,
-    wv, cpart, cbuf, wsend, wbuf, fsend, fbuf, gsend, gbuf, rbuf, pbuf, acc, coef, wide, dev_rows, dev_q, out,
-    w_sem, out_sem, c_send, c_recv, w_send, w_recv, f_send, f_recv, g_send, g_recv, r_send, r_recv, p_send, p_recv,
-    s_send, s_recv,
+    wv, cpart, cbuf, wsend, wbuf, fsend, fbuf, gsend, gbuf, rbuf, ybuf, pbuf, acc, coef, wide, dev_rows, dev_q, out,
+    w_sem, out_sem, c_send, c_recv, w_send, w_recv, f_send, f_recv, g_send, g_recv, r_send, r_recv, z_send, z_recv,
+    y_send, y_recv, x_send, x_recv, s_send, s_recv,
 ):
     row = lax.axis_index("row")
     col = lax.axis_index("col")
@@ -73,6 +73,13 @@
     panel_col = row // SUB
     sub = row % SUB
     is_self = panel_col == col
+    y, zl = row // 8, lax.rem(row // 2, 4)
+    x, zh = col // 2, lax.rem(col, 2)
+    half = zl // 2
+    in_half = half == zh
+
+    def dev(x, y, zh, zl):
+        return (lax.rem(y, 4) * 4 + lax.rem(zl, 4)) * 2 + core, lax.rem(x, 4) * 2 + zh
 
     w_copy = pltpu.make_async_copy(w_hbm, wv, w_sem)
     w_copy.start()
@@ -95,6 +102,8 @@
     lax.fori_loop(0, 32, greet_panel, 0)
     lax.fori_loop(1, COLS, lambda m, t: (greet(row, (col + m) % COLS), t)[1], 0)
     lax.fori_loop(1, ROWS, lambda m, t: (greet((row + m) % ROWS, col), t)[1], 0)
+    for i in range(1, 4):
+        greet(*dev(x, y, 1 - zh, zl + i))
 
     part = jnp.zeros((3, ATOMS_LOCAL), F32)
     for l in range(3):
@@ -111,9 +120,76 @@
     @pl.when(is_self)
     def _():
         cbuf[sub, col] = part
-        pbuf[sub, col] = x_ref[...]
-
-    pl.semaphore_wait(barrier, 70 - is_self.astype(jnp.int32))
+
+    @pl.when(in_half)
+    def _():
+        ybuf[y, 2 * (zl % 2) + zh] = x_ref[...]
+
+    pl.semaphore_wait(barrier, 73 - is_self.astype(jnp.int32))
+
+    def z_copy(i):
+        return remote(x_ref, ybuf.at[y, 2 * (zl % 2) + zh], z_send.at[i], z_recv.at[zl % 2, zh], *dev(x, y, half, zl + i))
+
+    def pair_copy():
+        return remote(x_ref, rbuf.at[col], z_send.at[0], r_recv.at[col], *dev(x, y, 1 - zh, zl))
+
+    def row_copy(i, other):
+        slot = 2 * x + (1 - zh if other else zh)
+        source = rbuf.at[slot] if other else x_ref
+        return remote(source, rbuf.at[slot], r_send.at[int(other), i], r_recv.at[slot], *dev(x + i, y, zh, zl))
+
+    def y_copy(i, k):
+        return remote(ybuf.at[y, k], ybuf.at[y, k], y_send.at[i, k], y_recv.at[y, k], *dev(x, y + i, zh, zl))
+
+    def x_copy(i, k):
+        there = lax.rem(x + i, 4)
+        return remote(ybuf.at[there, k], pbuf.at[core, k, x], x_send.at[i, k], x_recv.at[k, x], *dev(there, y, zh, zl))
+
+    def share_copy(k):
+        return remote(pbuf.at[core, k], pbuf.at[core, k], s_send.at[k], s_recv.at[k], sibling, col)
+
+    def chunk(n):
+        return 2 * (n % 2) + (zh if n < 2 else 1 - zh)
+
+    def y_step(n):
+        k = chunk(n)
+
+        @pl.when(jnp.logical_or(jnp.logical_not(in_half), zl % 2 != n % 2))
+        def _():
+            remote(x_ref, ybuf.at[y, k], z_send.at[0], z_recv.at[k // 2, k % 2], row, col).wait_recv()
+
+        for i in range(1, 4):
+            y_copy(i, k).start()
+
+    def x_step(n):
+        k = chunk(n)
+        for i in range(1, 4):
+            there = lax.rem(x + i, 4)
+
+            @pl.when(there != y)
+            def _():
+                remote(x_ref, ybuf.at[there, k], y_send.at[0, 0], y_recv.at[there, k], row, col).wait_recv()
+
+            x_copy(i, k).start()
+
+        @pl.when(x != y)
+        def _():
+            remote(x_ref, ybuf.at[x, k], y_send.at[0, 0], y_recv.at[x, k], row, col).wait_recv()
+
+        pbuf[core, k, x] = ybuf[x, k]
+
+    def share_step(n):
+        k = chunk(n)
+        for i in range(1, 4):
+            there = lax.rem(x + i, 4)
+            remote(x_ref, pbuf.at[core, k, there], x_send.at[0, 0], x_recv.at[k, there], row, col).wait_recv()
+        share_copy(k).start()
+
+    pair_copy().start()
+    for i in range(1, 4):
+        z_copy(i).start()
+    for i in range(1, 4):
+        row_copy(i, False).start()
 
     def centre_copy(m):
         r = (row + m) % ROWS
@@ -130,29 +206,17 @@
 
     lax.fori_loop(0, ROWS, centre_start, 0)
 
-    def row_copy(m):
-        c = (col + m) % COLS
-        return remote(x_ref, rbuf.at[col], r_send.at[m], r_recv.at[col], row, c)
-
-    def panel_copy(m):
-        r = 2 * ((row // 2 + m) % 16) + core
-        return r, remote(x_ref, pbuf.at[sub, col], p_send.at[m], p_recv.at[sub, col], r, panel_col)
-
-    def row_start(m, carry):
-        row_copy(m).start()
-        return carry
-
-    def panel_start(m, carry):
-        r, copy = panel_copy(m)
-
-        @pl.when(jnp.logical_or(r != row, jnp.logical_not(is_self)))
-        def _():
-            copy.start()
-
-        return carry
-
-    lax.fori_loop(1, COLS, row_start, 0)
-    lax.fori_loop(0, 16, panel_start, 0)
+    other_slot = 2 * x + 1 - zh
+    remote(x_ref, rbuf.at[other_slot], z_send.at[0], r_recv.at[other_slot], row, col).wait_recv()
+    for i in range(1, 4):
+        row_copy(i, True).start()
+
+    @pl.when(in_half)
+    def _():
+        ybuf[y, 2 * (zl % 2) + 1 - zh] = rbuf[other_slot]
+
+    for n in range(4):
+        y_step(n)
 
     def centre_wait(m, carry):
         q = m // COLS
@@ -206,6 +270,8 @@
         return carry
 
     lax.fori_loop(1, COLS, weight_start, 0)
+    x_step(0)
+    x_step(1)
     lax.fori_loop(1, COLS, weight_wait, 0)
     both = jnp.sum(wbuf[...], axis=0)
     centre_rows = both[3:6, :] * (1.0 / FRAMES)
@@ -230,6 +296,8 @@
         return carry
 
     lax.fori_loop(1, ROWS, fit_start, 0)
+    x_step(2)
+    x_step(3)
     lax.fori_loop(1, ROWS, fit_wait, 0)
     fitted = jnp.sum(fbuf[...], axis=0)
     gsend[...] = fitted
@@ -250,23 +318,8 @@
 
     lax.fori_loop(1, COLS, gather_start, 0)
 
-    def panel_wait(m, carry):
-        q = core + 2 * (m // COLS)
-        c = m % COLS
-
-        @pl.when(jnp.logical_or(SUB * col + q != row, c != col))
-        def _():
-            remote(x_ref, pbuf.at[q, c], p_send.at[0], p_recv.at[q, c], row, col).wait_recv()
-
-        return carry
-
-    def share_copy(j):
-        q = core + 2 * j
-        return remote(pbuf.at[q], pbuf.at[q], s_send.at[j], s_recv.at[q], sibling, col)
-
-    for j in range(2):
-        lax.fori_loop(j * COLS, (j + 1) * COLS, panel_wait, 0)
-        share_copy(j).start()
+    for n in range(4):
+        share_step(n)
 
     lax.fori_loop(1, COLS, gather_wait, 0)
 
@@ -281,18 +334,16 @@
             for c in range(COLS):
                 wide[3 * k + l, c] = jnp.broadcast_to(upright[0:FB, c : c + 1], (FB, 128))
 
-    def row_wait(m, carry):
-        c = (col + m) % COLS
-        remote(x_ref, rbuf.at[c], r_send.at[0], r_recv.at[c], row, col).wait_recv()
-        return carry
-
-    lax.fori_loop(1, COLS, row_wait, 0)
-
-    def deviate(source, centre):
+    for i in range(1, 4):
+        for h in range(2):
+            slot = 2 * lax.rem(x + i, 4) + h
+            remote(x_ref, rbuf.at[slot], r_send.at[0, 0], r_recv.at[slot], row, col).wait_recv()
+
+    def deviate(block_of, centre):
         base = [jnp.broadcast_to(centre[k : k + 1, :], (FB, ATOMS_LOCAL)) for k in range(3)]
 
         def body(c, carry):
-            block = source[c].astype(F32)
+            block = block_of(c).astype(F32)
             xs = [block[l * FB : (l + 1) * FB, :] for l in range(3)]
             start = pl.multiple_of(c * 96, 96)
             values = []
@@ -307,22 +358,25 @@
 
         lax.fori_loop(0, COLS, body, 0)
 
-    deviate(rbuf, centre_rows)
+    deviate(lambda c: rbuf[c], centre_rows)
     dev_rows[...] = jnp.transpose(dev_q[...])
 
-    for j in range(2):
-        q = 1 - core + 2 * j
-        remote(pbuf.at[q], pbuf.at[q], s_send.at[0], s_recv.at[q], row, col).wait_recv()
-
     def out_copy(q):
-        return pltpu.make_async_copy(
-            out.at[q], cov_hbm.at[:, pl.ds(pl.multiple_of(q * ATOMS_LOCAL, ATOMS_LOCAL), ATOMS_LOCAL)], out_sem.at[q]
-        )
-
-    for q in range(SUB):
-        deviate(pbuf.at[q], centre_cols[q])
-        out[q] = contract(dev_rows[...], dev_q[...], ((1,), (0,))) * (1.0 / (3 * FRAMES))
-        out_copy(q).start()
+        start = pl.multiple_of(q * ATOMS_LOCAL, ATOMS_LOCAL)
+        return pltpu.make_async_copy(out.at[q], cov_hbm.at[:, pl.ds(start, ATOMS_LOCAL)], out_sem.at[q])
+
+    for side in range(2):
+        owner = core if side == 0 else 1 - core
+        if side:
+            for n in range(4):
+                k = chunk(n)
+                remote(pbuf.at[owner, k], pbuf.at[owner, k], s_send.at[0], s_recv.at[k], row, col).wait_recv()
+        for j in range(2):
+            q = 2 * j + owner
+            centre_q = jnp.where(owner == 0, centre_cols[2 * j], centre_cols[2 * j + 1])
+            deviate(lambda c: pbuf[owner, 2 * j + lax.rem(c, 2), c // 2], centre_q)
+            out[q] = contract(dev_rows[...], dev_q[...], ((1,), (0,))) * (1.0 / (3 * FRAMES))
+            out_copy(q).start()
 
     for q in range(SUB):
         out_copy(q).wait()
@@ -336,21 +390,19 @@
 
         return carry
 
-    def panel_sent(m, carry):
-        r, copy = panel_copy(m)
-
-        @pl.when(jnp.logical_or(r != row, jnp.logical_not(is_self)))
-        def _():
-            copy.wait_send()
-
-        return carry
-
     lax.fori_loop(0, ROWS, centre_sent, 0)
-    lax.fori_loop(0, 16, panel_sent, 0)
-    for copy_of, count in ((row_copy, COLS), (weight_copy, COLS), (fit_copy, ROWS), (gather_copy, COLS)):
+    for copy_of, count in ((weight_copy, COLS), (fit_copy, ROWS), (gather_copy, COLS)):
         lax.fori_loop(1, count, lambda m, t, f=copy_of: (f(m).wait_send(), t)[1], 0)
-    for j in range(2):
-        share_copy(j).wait_send()
+    pair_copy().wait_send()
+    for i in range(1, 4):
+        z_copy(i).wait_send()
+        row_copy(i, False).wait_send()
+        row_copy(i, True).wait_send()
+        for k in range(4):
+            y_copy(i, k).wait_send()
+            x_copy(i, k).wait_send()
+    for k in range(4):
+        share_copy(k).wait_send()
 
 
 def per_device(frames, rotations, inverse_cov):
@@ -377,7 +429,8 @@
             pltpu.VMEM((3, 96), F32),
             pltpu.VMEM((8, 3, 96), F32),
             pltpu.VMEM((8, 96, 384), BF16),
-            pltpu.VMEM((4, 8, 96, 384), BF16),
+            pltpu.VMEM((4, 4, 96, 384), BF16),
+            pltpu.VMEM((2, 4, 4, 96, 384), BF16),
             pltpu.VMEM((3, 384, 128), F32),
             pltpu.VMEM((8, 128), F32),
             pltpu.VMEM((9, 8, 32, 128), F32),
@@ -389,9 +442,11 @@
             dma((8,)), dma((8,)),
             dma((32,)), dma((32,)),
             dma((8,)), dma((8,)),
-            dma((8,)), dma((8,)),
-            dma((16,)), dma((4, 8)),
-            dma((2,)), dma((4,)),
+            dma((2, 4)), dma((8,)),
+            dma((4,)), dma((2, 2)),
+            dma((4, 4)), dma((4, 4)),
+            dma((4, 4)), dma((4, 4)),
+            dma((4,)), dma((4,)),
         ],
         compiler_params=pltpu.CompilerParams(
             collective_id=0, has_side_effects=True, vmem_limit_bytes=48 * 1024 * 1024

time: 125 us -> 72.9 us (0.58)
  Pallas kernels: 119 us -> 66.8 us
    pallas_call x1, Pallas kernels: 119 us -> 66.8 us  [per_device(): pl.pallas_call(kernel, out_shape=(jax.ShapeDtypeStruct((ATOMS_LOCAL, SUB...]
where the time goes in v2:
time: 72.9 us; the launch traced here: 72.7 us
  Pallas kernels  66.8 us (92%)
  local copies, waits for them, and re-layouts  5.25 us (7%)
    pallas_call x1, Pallas kernels, per_device(): pl.pallas_call(kernel, out_shape=(jax.ShapeDtypeStruct((ATOMS_LOCAL, SUB...  66.8 us
    unnamed x8, local copies, waits for them, and re-layouts  5.25 us

profile of v2, /device:TPU:1, one launch (start us, length us, event | category | flops | bytes accessed | tf_op | source)
XLA Modules:
  0.0 72.7 jit_solution(16656491046360406446)
XLA Ops:
  0.6 0.0 copy-start
  0.6 1.7 %copy-done = f32[384,1536]{1,0:T(8,128)S(1)} copy-done((f32[384,1536]{1,0:T(8,128)S(1)}, f32[384,1536]{1,0:T(8,128)}, u32[]{:S(2)}) %copy-start) | copy-done | bytes 2359320
  2.3 0.0 copy-start.1
  2.3 0.9 %copy-done.1 = bf16[32,3,384]{2,0,1:T(8,128)(2,1)S(1)} copy-done((bf16[32,3,384]{2,0,1:T(8,128)(2,1)S(1)}, bf16[32,3,384]{2,0,1:T(8,128)(2,1)}, u32[]{:S(2)}) %copy-start.1) | copy-done | bytes 73752
  3.2 0.0 copy-start.2
  3.2 0.7 copy-done.2
  3.9 66.8 %superpose.1 = (f32[384,1536]{1,0:T(8,128)S(1)}, f32[3,3,32]{2,1,0:T(4,128)S(1)}) custom-call(bf16[96,384]{1,0:T(8,128)(2,1)S(1)} %bitcast.3, f32[3,3,256]{2,1,0:T(4,128)S(1)} %copy-done.2, f32[384,1536]{1,0:T(8,128)S(1)} %copy-done), custom_call_target="tpu_custom_call" | custom-call | tf_op jit(solution)/shard_map/superpose/pallas_call | solution.py:413
  70.7 1.4 %copy.7 = f32[384,1536]{1,0:T(8,128)} copy(f32[384,1536]{1,0:T(8,128)S(1)} %get-tuple-element.4) | data formatting | bytes 4718592
  72.1 0.6 copy.8
Async XLA Ops:
  0.6 1.7 %copy-start = (f32[384,1536]{1,0:T(8,128)S(1)}, f32[384,1536]{1,0:T(8,128)}, u32[]{:S(2)}) copy-start(f32[384,1536]{1,0:T(8,128)} %w_hbm.1) | copy-start | bytes 7077892
  2.3 0.9 %copy-start.1 = (bf16[32,3,384]{2,0,1:T(8,128)(2,1)S(1)}, bf16[32,3,384]{2,0,1:T(8,128)(2,1)}, u32[]{:S(2)}) copy-start(bf16[32,3,384]{2,0,1:T(8,128)(2,1)} %param.3) | copy-start | bytes 221188
  3.2 0.7 copy-start.2

commit v3 on v2

--- a/solution.py
+++ b/solution.py
@@ -61,9 +61,9 @@
 
 
 def kernel(
-    x_ref, rot_ref, w_hbm, cov_hbm, tr_ref,
-    wv, cpart, cbuf, wsend, wbuf, fsend, fbuf, gsend, gbuf, rbuf, ybuf, pbuf, acc, coef, wide, dev_rows, dev_q, out,
-    w_sem, out_sem, c_send, c_recv, w_send, w_recv, f_send, f_recv, g_send, g_recv, r_send, r_recv, z_send, z_recv,
+    x_hbm, rot_hbm, w_hbm, cov_hbm, tr_ref,
+    rot, wv, cpart, cbuf, asend, abuf, bsend, bbuf, rbuf, ybuf, pbuf, acc, coef, wide, dev_rows, dev_q, out,
+    in_sem, out_sem, c_send, c_recv, a_send, a_recv, b_send, b_recv, r_send, r_recv, z_send, z_recv,
     y_send, y_recv, x_send, x_recv, s_send, s_recv,
 ):
     row = lax.axis_index("row")
@@ -81,8 +81,23 @@
     def dev(x, y, zh, zl):
         return (lax.rem(y, 4) * 4 + lax.rem(zl, 4)) * 2 + core, lax.rem(x, 4) * 2 + zh
 
-    w_copy = pltpu.make_async_copy(w_hbm, wv, w_sem)
-    w_copy.start()
+    x_ref = rbuf.at[col]
+    x_load = pltpu.make_async_copy(x_hbm, x_ref, in_sem.at[0])
+    rot_load = pltpu.make_async_copy(rot_hbm, rot, in_sem.at[1])
+    w_load = pltpu.make_async_copy(w_hbm, wv, in_sem.at[2])
+    x_load.start()
+    rot_load.start()
+    w_load.start()
+
+    place = 2 * (4 * zh + zl) + core
+
+    def plane_peer(m):
+        return dev(x + m // 4, y + m % 4, zh, zl)
+
+    def ring_peer(m):
+        there = lax.rem(place + m, 16)
+        zc = there // 2
+        return (y * 4 + lax.rem(zc, 4)) * 2 + lax.rem(there, 2), 2 * x + zc // 4
 
     barrier = pltpu.get_barrier_semaphore()
 
@@ -91,7 +106,7 @@
 
     def greet_panel(m, carry):
         r = SUB * col + m // COLS
-        c = m % COLS
+        c = lax.rem(m, COLS)
 
         @pl.when(jnp.logical_or(r != row, c != col))
         def _():
@@ -100,14 +115,15 @@
         return carry
 
     lax.fori_loop(0, 32, greet_panel, 0)
-    lax.fori_loop(1, COLS, lambda m, t: (greet(row, (col + m) % COLS), t)[1], 0)
-    lax.fori_loop(1, ROWS, lambda m, t: (greet((row + m) % ROWS, col), t)[1], 0)
-    for i in range(1, 4):
-        greet(*dev(x, y, 1 - zh, zl + i))
-
+    for m in range(1, 16):
+        greet(*plane_peer(m))
+        greet(*ring_peer(m))
+
+    x_load.wait()
+    rot_load.wait()
     part = jnp.zeros((3, ATOMS_LOCAL), F32)
     for l in range(3):
-        whole = rot_ref[:, l, :]
+        whole = rot[:, l, :]
         mine = jnp.zeros((3, FB), F32)
         for i in range(COLS):
             mine = mine + jnp.where(col == i, whole[:, i * FB : (i + 1) * FB], 0.0)
@@ -115,7 +131,6 @@
         for piece in split3(mine):
             part = part + contract(piece, block, ((1,), (0,)))
     cpart[...] = part
-    rbuf[col] = x_ref[...]
 
     @pl.when(is_self)
     def _():
@@ -125,7 +140,7 @@
     def _():
         ybuf[y, 2 * (zl % 2) + zh] = x_ref[...]
 
-    pl.semaphore_wait(barrier, 73 - is_self.astype(jnp.int32))
+    pl.semaphore_wait(barrier, 62 - is_self.astype(jnp.int32))
 
     def z_copy(i):
         return remote(x_ref, ybuf.at[y, 2 * (zl % 2) + zh], z_send.at[i], z_recv.at[zl % 2, zh], *dev(x, y, half, zl + i))
@@ -231,7 +246,7 @@
     lax.fori_loop(0, SUB * COLS, centre_wait, 0)
     centre_cols = jnp.sum(cbuf[...], axis=1) * (1.0 / FRAMES)
 
-    w_copy.wait()
+    w_load.wait()
     lanes = [[centre_cols[q][l : l + 1, :] for q in range(SUB)] for l in range(3)]
 
     def weigh(i, carry):
@@ -243,101 +258,79 @@
                 for l in range(3):
                     sums[l] = sums[l] + tile * lanes[l][q][:, t * 128 : (t + 1) * 128]
         for l in range(3):
-            acc[l, pl.ds(start, 32), :] = sums[l]
+            for p, piece in enumerate(split3(sums[l])):
+                acc[pl.ds(start, 32), (3 * l + p) * 128 : (3 * l + p + 1) * 128] = piece
         return carry
 
     lax.fori_loop(0, 12, weigh, 0)
-    ones = jnp.ones((8, 128), BF16)
-    for l in range(3):
-        line = jnp.zeros((8, ATOMS_LOCAL), F32)
-        for piece in split3(acc[l]):
-            line = line + contract(ones, piece, ((1,), (1,)))
-        wsend[l : l + 1, :] = line[0:1, :]
-    wsend[3:6, :] = cpart[...]
-    wbuf[col] = wsend[...]
-
-    def weight_copy(m):
-        c = (col + m) % COLS
-        return remote(wsend, wbuf.at[col], w_send.at[m], w_recv.at[col], row, c)
-
-    def weight_start(m, carry):
-        weight_copy(m).start()
-        return carry
-
-    def weight_wait(m, carry):
-        c = (col + m) % COLS
-        remote(wsend, wbuf.at[c], w_send.at[0], w_recv.at[c], row, col).wait_recv()
-        return carry
-
-    lax.fori_loop(1, COLS, weight_start, 0)
-    x_step(0)
-    x_step(1)
-    lax.fori_loop(1, COLS, weight_wait, 0)
-    both = jnp.sum(wbuf[...], axis=0)
-    centre_rows = both[3:6, :] * (1.0 / FRAMES)
-
-    fit = jnp.zeros((3, 96), F32)
-    for piece in split3(both[0:3, :]):
-        fit = fit + contract(piece, x_ref[...], ((1,), (1,)))
-    fsend[...] = fit
-    fbuf[row] = fit
-
-    def fit_copy(m):
-        r = (row + m) % ROWS
-        return remote(fsend, fbuf.at[row], f_send.at[m], f_recv.at[row], r, col)
-
-    def fit_start(m, carry):
-        fit_copy(m).start()
-        return carry
-
-    def fit_wait(m, carry):
-        r = (row + m) % ROWS
-        remote(fsend, fbuf.at[r], f_send.at[0], f_recv.at[r], row, col).wait_recv()
-        return carry
-
-    lax.fori_loop(1, ROWS, fit_start, 0)
-    x_step(2)
-    x_step(3)
-    lax.fori_loop(1, ROWS, fit_wait, 0)
-    fitted = jnp.sum(fbuf[...], axis=0)
-    gsend[...] = fitted
-    gbuf[col] = fitted
-
-    def gather_copy(m):
-        c = (col + m) % COLS
-        return remote(gsend, gbuf.at[col], g_send.at[m], g_recv.at[col], row, c)
-
-    def gather_start(m, carry):
-        gather_copy(m).start()
-        return carry
-
-    def gather_wait(m, carry):
-        c = (col + m) % COLS
-        remote(gsend, gbuf.at[c], g_send.at[0], g_recv.at[c], row, col).wait_recv()
-        return carry
-
-    lax.fori_loop(1, COLS, gather_start, 0)
-
-    for n in range(4):
-        share_step(n)
-
-    lax.fori_loop(1, COLS, gather_wait, 0)
-
-    rows_of = [gbuf[:, l, :] for l in range(3)]
-    turned = polar_all([[rows_of[l][:, k * FB : (k + 1) * FB] for l in range(3)] for k in range(3)])
-    at_col = lax.broadcasted_iota(jnp.int32, (COLS, FB), 0) == col
-    for k in range(3):
-        for l in range(3):
-            tr_ref[k, l : l + 1, :] = jnp.sum(jnp.where(at_col, turned[k][l], 0.0), axis=0, keepdims=True)
-            coef[:, 0:FB] = turned[k][l]
-            upright = jnp.transpose(coef[...])
-            for c in range(COLS):
-                wide[3 * k + l, c] = jnp.broadcast_to(upright[0:FB, c : c + 1], (FB, 128))
+    shape = (8, 9 * 128)
+    owner_of = lax.broadcasted_iota(jnp.int32, shape, 1) // 384
+    chooser = jnp.where(owner_of == lax.broadcasted_iota(jnp.int32, shape, 0), 1.0, 0.0).astype(BF16)
+    weighted = contract(chooser, acc[...], ((1,), (1,)))
 
     for i in range(1, 4):
         for h in range(2):
             slot = 2 * lax.rem(x + i, 4) + h
             remote(x_ref, rbuf.at[slot], r_send.at[0, 0], r_recv.at[slot], row, col).wait_recv()
+    pieces = jnp.concatenate(split3(weighted), axis=0)
+    for k in range(3):
+        frames_k = rbuf[:, k * FB : (k + 1) * FB, :].reshape(FRAMES, ATOMS_LOCAL)
+        product = contract(pieces, frames_k, ((1,), (1,)))
+        asend[k] = (product[0:8] + product[8:16] + product[16:24])[0:3]
+    a_slot = 4 * x + y
+    abuf[a_slot] = asend[...]
+
+    def plane_copy(m):
+        return remote(asend, abuf.at[a_slot], a_send.at[m], a_recv.at[a_slot], *plane_peer(m))
+
+    def ring_copy(m):
+        return remote(bsend, bbuf.at[place], b_send.at[m], b_recv.at[place], *ring_peer(m))
+
+    for m in range(1, 16):
+        plane_copy(m).start()
+    x_step(0)
+    x_step(1)
+    for m in range(1, 16):
+        slot = 4 * lax.rem(x + m // 4, 4) + lax.rem(y + m % 4, 4)
+        remote(asend, abuf.at[slot], a_send.at[0], a_recv.at[slot], row, col).wait_recv()
+    partial_fit = jnp.sum(abuf[...], axis=0)
+    bsend[...] = partial_fit
+    bbuf[place] = partial_fit
+    for m in range(1, 16):
+        ring_copy(m).start()
+    x_step(2)
+    x_step(3)
+
+    centre_rows = jnp.zeros((8, ATOMS_LOCAL), F32)
+    for l in range(3):
+        frames_l = rbuf[:, l * FB : (l + 1) * FB, :].reshape(FRAMES, ATOMS_LOCAL)
+        spin = jnp.concatenate([rot[:, l, :], jnp.zeros((5, FRAMES), F32)], axis=0)
+        product = contract(jnp.concatenate(split3(spin), axis=0), frames_l, ((1,), (0,)))
+        centre_rows = centre_rows + (product[0:8] + product[8:16] + product[16:24])
+    centre_rows = centre_rows * (1.0 / FRAMES)
+
+    for n in range(4):
+        share_step(n)
+
+    for m in range(1, 16):
+        slot = lax.rem(place + m, 16)
+        remote(bsend, bbuf.at[slot], b_send.at[0], b_recv.at[slot], row, col).wait_recv()
+    fitted = jnp.sum(bbuf[...], axis=0)
+
+    turned = polar_all([[fitted[k][l : l + 1, :] for l in range(3)] for k in range(3)])
+    for k in range(3):
+        for l in range(3):
+            coef[3 * k + l : 3 * k + l + 1, :] = turned[k][l]
+    every = coef[...]
+    mine = jnp.zeros((16, FB), F32)
+    for i in range(COLS):
+        mine = mine + jnp.where(col == i, every[:, i * FB : (i + 1) * FB], 0.0)
+    for k in range(3):
+        tr_ref[k] = mine[3 * k : 3 * k + 3, :]
+    upright = jnp.transpose(every)
+    for c in range(COLS):
+        for j in range(9):
+            wide[j, c] = jnp.broadcast_to(upright[c * FB : (c + 1) * FB, j : j + 1], (FB, 128))
 
     def deviate(block_of, centre):
         base = [jnp.broadcast_to(centre[k : k + 1, :], (FB, ATOMS_LOCAL)) for k in range(3)]
@@ -391,8 +384,9 @@
         return carry
 
     lax.fori_loop(0, ROWS, centre_sent, 0)
-    for copy_of, count in ((weight_copy, COLS), (fit_copy, ROWS), (gather_copy, COLS)):
-        lax.fori_loop(1, count, lambda m, t, f=copy_of: (f(m).wait_send(), t)[1], 0)
+    for m in range(1, 16):
+        plane_copy(m).wait_send()
+        ring_copy(m).wait_send()
     pair_copy().wait_send()
     for i in range(1, 4):
         z_copy(i).wait_send()
@@ -409,39 +403,37 @@
     x = jnp.transpose(frames, (1, 0, 2)).reshape(96, ATOMS_LOCAL)
     dma = pltpu.SemaphoreType.DMA
     vmem = pl.BlockSpec(memory_space=pltpu.VMEM)
-    hbm = pl.BlockSpec(memory_space=pl.ANY)
+    hbm = pl.BlockSpec(memory_space=pltpu.HBM)
     return pl.pallas_call(
         kernel,
         out_shape=(
             jax.ShapeDtypeStruct((ATOMS_LOCAL, SUB * ATOMS_LOCAL), F32),
             jax.ShapeDtypeStruct((3, 3, FB), F32),
         ),
-        in_specs=[vmem, vmem, hbm],
-        out_specs=(hbm, vmem),
+        in_specs=[hbm, hbm, hbm],
+        out_specs=(pl.BlockSpec(memory_space=pl.ANY), vmem),
         scratch_shapes=[
+            pltpu.VMEM((3, 3, 256), F32),
             pltpu.VMEM((384, 1536), F32),
             pltpu.VMEM((3, 384), F32),
             pltpu.VMEM((4, 8, 3, 384), F32),
-            pltpu.VMEM((6, 384), F32),
-            pltpu.VMEM((8, 6, 384), F32),
-            pltpu.VMEM((3, 96), F32),
-            pltpu.VMEM((32, 3, 96), F32),
-            pltpu.VMEM((3, 96), F32),
-            pltpu.VMEM((8, 3, 96), F32),
+            pltpu.VMEM((3, 3, 256), F32),
+            pltpu.VMEM((16, 3, 3, 256), F32),
+            pltpu.VMEM((3, 3, 256), F32),
+            pltpu.VMEM((16, 3, 3, 256), F32),
             pltpu.VMEM((8, 96, 384), BF16),
             pltpu.VMEM((4, 4, 96, 384), BF16),
             pltpu.VMEM((2, 4, 4, 96, 384), BF16),
-            pltpu.VMEM((3, 384, 128), F32),
-            pltpu.VMEM((8, 128), F32),
+            pltpu.VMEM((384, 1152), BF16),
+            pltpu.VMEM((16, 256), F32),
             pltpu.VMEM((9, 8, 32, 128), F32),
             pltpu.VMEM((384, 768), BF16),
             pltpu.VMEM((768, 384), BF16),
             pltpu.VMEM((4, 384, 384), F32),
-            dma(()), dma((4,)),
+            dma((3,)), dma((4,)),
             dma((32,)), dma((4, 8)),
-            dma((8,)), dma((8,)),
-            dma((32,)), dma((32,)),
-            dma((8,)), dma((8,)),
+            dma((16,)), dma((16,)),
+            dma((16,)), dma((16,)),
             dma((2, 4)), dma((8,)),
             dma((4,)), dma((2, 2)),
             dma((4, 4)), dma((4, 4)),

time: 72.9 us -> 67.8 us (0.930)
  the two profiles are of different devices: /device:TPU:1 before, /device:TPU:96 now
where the time goes in v3:
time: 67.8 us; the launch traced here: 67.6 us
  Pallas kernels  61.7 us (91%)
  local copies, waits for them, and re-layouts  5.25 us (8%)
    pallas_call x1, Pallas kernels, per_device(): pl.pallas_call(kernel, out_shape=(jax.ShapeDtypeStruct((ATOMS_LOCAL, SUB...  61.7 us
    unnamed x8, local copies, waits for them, and re-layouts  5.25 us

profile of v3, /device:TPU:96, one launch (start us, length us, event | category | flops | bytes accessed | tf_op | source)
XLA Modules:
  0.0 67.6 jit_solution(2505317007759492325)
XLA Ops:
  0.6 0.0 copy-start
  0.6 1.7 %copy-done = f32[384,1536]{1,0:T(8,128)S(1)} copy-done((f32[384,1536]{1,0:T(8,128)S(1)}, f32[384,1536]{1,0:T(8,128)}, u32[]{:S(2)}) %copy-start) | copy-done | bytes 2359320
  2.3 0.0 copy-start.1
  2.3 0.9 %copy-done.1 = bf16[32,3,384]{2,0,1:T(8,128)(2,1)S(1)} copy-done((bf16[32,3,384]{2,0,1:T(8,128)(2,1)S(1)}, bf16[32,3,384]{2,0,1:T(8,128)(2,1)}, u32[]{:S(2)}) %copy-start.1) | copy-done | bytes 73752
  3.2 0.0 copy-start.2
  3.2 0.7 %copy-done.2 = f32[3,3,256]{2,1,0:T(4,128)S(1)} copy-done((f32[3,3,256]{2,1,0:T(4,128)S(1)}, f32[3,3,256]{2,1,0:T(4,128)}, u32[]{:S(2)}) %copy-start.2) | copy-done | bytes 9240
  3.9 61.7 %superpose.1 = (f32[384,1536]{1,0:T(8,128)S(1)}, f32[3,3,32]{2,1,0:T(4,128)S(1)}) custom-call(bf16[96,384]{1,0:T(8,128)(2,1)S(1)} %bitcast.3, f32[3,3,256]{2,1,0:T(4,128)S(1)} %copy-done.2, f32[384,1536]{1,0:T(8,128)S(1)} %copy-done), custom_call_target="tpu_custom_call" | custom-call | tf_op jit(solution)/shard_map/superpose/pallas_call | solution.py:407
  65.6 1.4 %copy.7 = f32[384,1536]{1,0:T(8,128)} copy(f32[384,1536]{1,0:T(8,128)S(1)} %get-tuple-element.4) | data formatting | bytes 4718592
  67.0 0.6 copy.8
Async XLA Ops:
  0.6 1.7 %copy-start = (f32[384,1536]{1,0:T(8,128)S(1)}, f32[384,1536]{1,0:T(8,128)}, u32[]{:S(2)}) copy-start(f32[384,1536]{1,0:T(8,128)} %w_hbm.1) | copy-start | bytes 7077892
  2.3 0.9 %copy-start.1 = (bf16[32,3,384]{2,0,1:T(8,128)(2,1)S(1)}, bf16[32,3,384]{2,0,1:T(8,128)(2,1)}, u32[]{:S(2)}) copy-start(bf16[32,3,384]{2,0,1:T(8,128)(2,1)} %param.3) | copy-start | bytes 221188
  3.2 0.7 %copy-start.2 = (f32[3,3,256]{2,1,0:T(4,128)S(1)}, f32[3,3,256]{2,1,0:T(4,128)}, u32[]{:S(2)}) copy-start(f32[3,3,256]{2,1,0:T(4,128)} %rot_hbm.1) | copy-start | bytes 27652

commit v4 on v3

--- a/solution.py
+++ b/solution.py
@@ -62,8 +62,8 @@
 
 def kernel(
     x_hbm, rot_hbm, w_hbm, cov_hbm, tr_ref,
-    rot, wv, cpart, cbuf, asend, abuf, bsend, bbuf, rbuf, ybuf, pbuf, acc, coef, wide, dev_rows, dev_q, out,
-    in_sem, out_sem, c_send, c_recv, a_send, a_recv, b_send, b_recv, r_send, r_recv, z_send, z_recv,
+    rot, wv, cpart, cbuf, csum, hsend, hbuf, asend, abuf, bsend, bbuf, turn, rbuf, ybuf, pbuf, acc, coef, wide, dev_rows, dev_q, out,
+    in_sem, out_sem, c_send, c_recv, h_send, h_recv, a_send, a_recv, b_send, b_recv, r_send, r_recv, z_send, z_recv,
     y_send, y_recv, x_send, x_recv, s_send, s_recv,
 ):
     row = lax.axis_index("row")
@@ -89,35 +89,33 @@
     rot_load.start()
     w_load.start()
 
-    place = 2 * (4 * zh + zl) + core
+    z = 4 * zh + zl
 
     def plane_peer(m):
         return dev(x + m // 4, y + m % 4, zh, zl)
 
     def ring_peer(m):
-        there = lax.rem(place + m, 16)
-        zc = there // 2
-        return (y * 4 + lax.rem(zc, 4)) * 2 + lax.rem(there, 2), 2 * x + zc // 4
+        there = lax.rem(z + m, 8)
+        return dev(x, y, there // 4, there)
 
     barrier = pltpu.get_barrier_semaphore()
 
     def greet(r, c):
         pl.semaphore_signal(barrier, inc=1, device_id=(r, c), device_id_type=MESH)
 
-    def greet_panel(m, carry):
-        r = SUB * col + m // COLS
-        c = lax.rem(m, COLS)
+    for m in range(16):
+        r = SUB * col + 2 * (m // COLS) + core
+        c = m % COLS
 
         @pl.when(jnp.logical_or(r != row, c != col))
         def _():
             greet(r, c)
 
-        return carry
-
-    lax.fori_loop(0, 32, greet_panel, 0)
     for m in range(1, 16):
         greet(*plane_peer(m))
+    for m in range(1, 8):
         greet(*ring_peer(m))
+    greet(sibling, col)
 
     x_load.wait()
     rot_load.wait()
@@ -130,17 +128,18 @@
         block = x_ref[l * FB : (l + 1) * FB, :]
         for piece in split3(mine):
             part = part + contract(piece, block, ((1,), (0,)))
-    cpart[...] = part
+    for l in range(3):
+        cpart[0:1, l * ATOMS_LOCAL : (l + 1) * ATOMS_LOCAL] = part[l : l + 1, :]
 
     @pl.when(is_self)
     def _():
-        cbuf[sub, col] = part
+        cbuf[sub // 2, col] = cpart[...]
 
     @pl.when(in_half)
     def _():
         ybuf[y, 2 * (zl % 2) + zh] = x_ref[...]
 
-    pl.semaphore_wait(barrier, 62 - is_self.astype(jnp.int32))
+    pl.semaphore_wait(barrier, 39 - is_self.astype(jnp.int32))
 
     def z_copy(i):
         return remote(x_ref, ybuf.at[y, 2 * (zl % 2) + zh], z_send.at[i], z_recv.at[zl % 2, zh], *dev(x, y, half, zl + i))
@@ -207,19 +206,17 @@
         row_copy(i, False).start()
 
     def centre_copy(m):
-        r = (row + m) % ROWS
-        return r, remote(cpart, cbuf.at[sub, col], c_send.at[m], c_recv.at[sub, col], r, panel_col)
-
-    def centre_start(m, carry):
-        r, copy = centre_copy(m)
-
-        @pl.when(jnp.logical_or(r != row, jnp.logical_not(is_self)))
-        def _():
-            copy.start()
-
-        return carry
-
-    lax.fori_loop(0, ROWS, centre_start, 0)
+        r = 2 * lax.rem(row // 2 + m, 16) + core
+        return remote(cpart, cbuf.at[sub // 2, col], c_send.at[m], c_recv.at[sub // 2, col], r, panel_col)
+
+    for m in range(16):
+        if m:
+            centre_copy(m).start()
+        else:
+
+            @pl.when(jnp.logical_not(is_self))
+            def _():
+                centre_copy(0).start()
 
     other_slot = 2 * x + 1 - zh
     remote(x_ref, rbuf.at[other_slot], z_send.at[0], r_recv.at[other_slot], row, col).wait_recv()
@@ -230,24 +227,29 @@
     def _():
         ybuf[y, 2 * (zl % 2) + 1 - zh] = rbuf[other_slot]
 
-    for n in range(4):
-        y_step(n)
-
-    def centre_wait(m, carry):
-        q = m // COLS
-        c = m % COLS
-
-        @pl.when(jnp.logical_or(SUB * col + q != row, c != col))
-        def _():
-            remote(cpart, cbuf.at[q, c], c_send.at[0], c_recv.at[q, c], row, col).wait_recv()
-
-        return carry
-
-    lax.fori_loop(0, SUB * COLS, centre_wait, 0)
-    centre_cols = jnp.sum(cbuf[...], axis=1) * (1.0 / FRAMES)
+    y_step(0)
+    y_step(1)
+
+    for j in range(2):
+        for c in range(COLS):
+
+            @pl.when(jnp.logical_or(SUB * col + 2 * j + core != row, c != col))
+            def _():
+                remote(cpart, cbuf.at[j, c], c_send.at[0], c_recv.at[j, c], row, col).wait_recv()
+
+    csum[core] = jnp.sum(cbuf[...], axis=1) * (1.0 / FRAMES)
+
+    def half_copy(i, src, dst):
+        return remote(src, dst, h_send.at[i], h_recv.at[i], sibling, col)
+
+    centre_half = half_copy(0, csum.at[core], csum.at[core])
+    centre_half.start()
+    y_step(2)
+    y_step(3)
+    half_copy(0, csum.at[core], csum.at[1 - core]).wait_recv()
 
     w_load.wait()
-    lanes = [[centre_cols[q][l : l + 1, :] for q in range(SUB)] for l in range(3)]
+    lanes = [[csum[q % 2, q // 2, :, l * ATOMS_LOCAL : (l + 1) * ATOMS_LOCAL] for q in range(SUB)] for l in range(3)]
 
     def weigh(i, carry):
         start = pl.multiple_of(i * 32, 32)
@@ -273,10 +275,22 @@
             slot = 2 * lax.rem(x + i, 4) + h
             remote(x_ref, rbuf.at[slot], r_send.at[0, 0], r_recv.at[slot], row, col).wait_recv()
     pieces = jnp.concatenate(split3(weighted), axis=0)
+    first = core == 0
     for k in range(3):
         frames_k = rbuf[:, k * FB : (k + 1) * FB, :].reshape(FRAMES, ATOMS_LOCAL)
         product = contract(pieces, frames_k, ((1,), (1,)))
-        asend[k] = (product[0:8] + product[8:16] + product[16:24])[0:3]
+        product = product[0:8] + product[8:16] + product[16:24]
+        own = jnp.where(first, product[:, 0:128], product[:, 128:256])
+        others = jnp.where(first, product[:, 128:256], product[:, 0:128])
+        for l in range(3):
+            at = (3 * k + l) * 128
+            asend[0:1, at : at + 128] = own[l : l + 1, :]
+            hsend[0:1, at : at + 128] = others[l : l + 1, :]
+    fit_half = half_copy(1, hsend, hbuf.at[0])
+    fit_half.start()
+    x_step(0)
+    fit_half.wait_recv()
+    asend[...] = asend[...] + hbuf[0]
     a_slot = 4 * x + y
     abuf[a_slot] = asend[...]
 
@@ -284,22 +298,22 @@
         return remote(asend, abuf.at[a_slot], a_send.at[m], a_recv.at[a_slot], *plane_peer(m))
 
     def ring_copy(m):
-        return remote(bsend, bbuf.at[place], b_send.at[m], b_recv.at[place], *ring_peer(m))
+        return remote(bsend, bbuf.at[z], b_send.at[m], b_recv.at[z], *ring_peer(m))
 
     for m in range(1, 16):
         plane_copy(m).start()
-    x_step(0)
     x_step(1)
     for m in range(1, 16):
         slot = 4 * lax.rem(x + m // 4, 4) + lax.rem(y + m % 4, 4)
         remote(asend, abuf.at[slot], a_send.at[0], a_recv.at[slot], row, col).wait_recv()
-    partial_fit = jnp.sum(abuf[...], axis=0)
-    bsend[...] = partial_fit
-    bbuf[place] = partial_fit
-    for m in range(1, 16):
+    bsend[...] = jnp.sum(abuf[...], axis=0)
+    bbuf[z] = bsend[...]
+    for m in range(1, 8):
         ring_copy(m).start()
     x_step(2)
     x_step(3)
+    share_step(0)
+    share_step(1)
 
     centre_rows = jnp.zeros((8, ATOMS_LOCAL), F32)
     for l in range(3):
@@ -309,31 +323,38 @@
         centre_rows = centre_rows + (product[0:8] + product[8:16] + product[16:24])
     centre_rows = centre_rows * (1.0 / FRAMES)
 
-    for n in range(4):
-        share_step(n)
-
-    for m in range(1, 16):
-        slot = lax.rem(place + m, 16)
+    for m in range(1, 8):
+        slot = lax.rem(z + m, 8)
         remote(bsend, bbuf.at[slot], b_send.at[0], b_recv.at[slot], row, col).wait_recv()
     fitted = jnp.sum(bbuf[...], axis=0)
 
-    turned = polar_all([[fitted[k][l : l + 1, :] for l in range(3)] for k in range(3)])
+    turned = polar_all([[fitted[:, (3 * k + l) * 128 : (3 * k + l + 1) * 128] for l in range(3)] for k in range(3)])
     for k in range(3):
         for l in range(3):
-            coef[3 * k + l : 3 * k + l + 1, :] = turned[k][l]
-    every = coef[...]
-    mine = jnp.zeros((16, FB), F32)
-    for i in range(COLS):
-        mine = mine + jnp.where(col == i, every[:, i * FB : (i + 1) * FB], 0.0)
+            turn[core, :, (3 * k + l) * 128 : (3 * k + l + 1) * 128] = turned[k][l]
+    turn_half = half_copy(2, turn.at[core], turn.at[core])
+    turn_half.start()
+    share_step(2)
+    half_copy(2, turn.at[core], turn.at[1 - core]).wait_recv()
+    picked = jnp.where(col < 4, turn[0], turn[1])
+    quarter = lax.rem(col, 4)
     for k in range(3):
-        tr_ref[k] = mine[3 * k : 3 * k + 3, :]
-    upright = jnp.transpose(every)
-    for c in range(COLS):
+        for l in range(3):
+            line = picked[:, (3 * k + l) * 128 : (3 * k + l + 1) * 128]
+            mine = jnp.zeros((1, FB), F32)
+            for i in range(4):
+                mine = mine + jnp.where(quarter == i, line[:, i * FB : (i + 1) * FB], 0.0)
+            tr_ref[k, l : l + 1, :] = mine
+    for half_of in range(2):
         for j in range(9):
-            wide[j, c] = jnp.broadcast_to(upright[c * FB : (c + 1) * FB, j : j + 1], (FB, 128))
+            coef[j : j + 1, :] = turn[half_of, :, j * 128 : (j + 1) * 128]
+        upright = jnp.transpose(coef[...])
+        for c in range(4):
+            for j in range(9):
+                wide[j, 4 * half_of + c] = jnp.broadcast_to(upright[c * FB : (c + 1) * FB, j : j + 1], (FB, 128))
 
     def deviate(block_of, centre):
-        base = [jnp.broadcast_to(centre[k : k + 1, :], (FB, ATOMS_LOCAL)) for k in range(3)]
+        base = [jnp.broadcast_to(centre[k], (FB, ATOMS_LOCAL)) for k in range(3)]
 
         def body(c, carry):
             block = block_of(c).astype(F32)
@@ -351,8 +372,9 @@
 
         lax.fori_loop(0, COLS, body, 0)
 
-    deviate(lambda c: rbuf[c], centre_rows)
+    deviate(lambda c: rbuf[c], [centre_rows[k : k + 1, :] for k in range(3)])
     dev_rows[...] = jnp.transpose(dev_q[...])
+    share_step(3)
 
     def out_copy(q):
         start = pl.multiple_of(q * ATOMS_LOCAL, ATOMS_LOCAL)
@@ -360,13 +382,13 @@
 
     for side in range(2):
         owner = core if side == 0 else 1 - core
-        if side:
-            for n in range(4):
-                k = chunk(n)
-                remote(pbuf.at[owner, k], pbuf.at[owner, k], s_send.at[0], s_recv.at[k], row, col).wait_recv()
         for j in range(2):
+            if side:
+                for h in range(2):
+                    k = 2 * j + h
+                    remote(pbuf.at[owner, k], pbuf.at[owner, k], s_send.at[0], s_recv.at[k], row, col).wait_recv()
             q = 2 * j + owner
-            centre_q = jnp.where(owner == 0, centre_cols[2 * j], centre_cols[2 * j + 1])
+            centre_q = [csum[owner, j, :, k * ATOMS_LOCAL : (k + 1) * ATOMS_LOCAL] for k in range(3)]
             deviate(lambda c: pbuf[owner, 2 * j + lax.rem(c, 2), c // 2], centre_q)
             out[q] = contract(dev_rows[...], dev_q[...], ((1,), (0,))) * (1.0 / (3 * FRAMES))
             out_copy(q).start()
@@ -374,19 +396,22 @@
     for q in range(SUB):
         out_copy(q).wait()
 
-    def centre_sent(m, carry):
-        r, copy = centre_copy(m)
-
-        @pl.when(jnp.logical_or(r != row, jnp.logical_not(is_self)))
-        def _():
-            copy.wait_send()
-
-        return carry
-
-    lax.fori_loop(0, ROWS, centre_sent, 0)
+    for m in range(16):
+        if m:
+            centre_copy(m).wait_send()
+        else:
+
+            @pl.when(jnp.logical_not(is_self))
+            def _():
+                centre_copy(0).wait_send()
+
     for m in range(1, 16):
         plane_copy(m).wait_send()
+    for m in range(1, 8):
         ring_copy(m).wait_send()
+    centre_half.wait_send()
+    fit_half.wait_send()
+    turn_half.wait_send()
     pair_copy().wait_send()
     for i in range(1, 4):
         z_copy(i).wait_send()
@@ -415,25 +440,30 @@
         scratch_shapes=[
             pltpu.VMEM((3, 3, 256), F32),
             pltpu.VMEM((384, 1536), F32),
-            pltpu.VMEM((3, 384), F32),
-            pltpu.VMEM((4, 8, 3, 384), F32),
-            pltpu.VMEM((3, 3, 256), F32),
-            pltpu.VMEM((16, 3, 3, 256), F32),
-            pltpu.VMEM((3, 3, 256), F32),
-            pltpu.VMEM((16, 3, 3, 256), F32),
+            pltpu.VMEM((1, 1152), F32),
+            pltpu.VMEM((2, 8, 1, 1152), F32),
+            pltpu.VMEM((2, 2, 1, 1152), F32),
+            pltpu.VMEM((1, 1152), F32),
+            pltpu.VMEM((1, 1, 1152), F32),
+            pltpu.VMEM((1, 1152), F32),
+            pltpu.VMEM((16, 1, 1152), F32),
+            pltpu.VMEM((1, 1152), F32),
+            pltpu.VMEM((8, 1, 1152), F32),
+            pltpu.VMEM((2, 1, 1152), F32),
             pltpu.VMEM((8, 96, 384), BF16),
             pltpu.VMEM((4, 4, 96, 384), BF16),
             pltpu.VMEM((2, 4, 4, 96, 384), BF16),
             pltpu.VMEM((384, 1152), BF16),
-            pltpu.VMEM((16, 256), F32),
+            pltpu.VMEM((16, 128), F32),
             pltpu.VMEM((9, 8, 32, 128), F32),
             pltpu.VMEM((384, 768), BF16),
             pltpu.VMEM((768, 384), BF16),
             pltpu.VMEM((4, 384, 384), F32),
             dma((3,)), dma((4,)),
-            dma((32,)), dma((4, 8)),
+            dma((16,)), dma((2, 8)),
+            dma((3,)), dma((3,)),
             dma((16,)), dma((16,)),
-            dma((16,)), dma((16,)),
+            dma((8,)), dma((8,)),
             dma((2, 4)), dma((8,)),
             dma((4,)), dma((2, 2)),
             dma((4, 4)), dma((4, 4)),
@@ -441,7 +471,7 @@
             dma((4,)), dma((4,)),
         ],
         compiler_params=pltpu.CompilerParams(
-            collective_id=0, has_side_effects=True, vmem_limit_bytes=48 * 1024 * 1024
+            collective_id=0, has_side_effects=True, vmem_limit_bytes=56 * 1024 * 1024
         ),
         name="superpose",
     )(x, rotations, inverse_cov)

time: 67.8 us -> 58.2 us (0.86)
  the two profiles are of different devices: /device:TPU:96 before, /device:TPU:1 now
where the time goes in v4:
time: 58.2 us; the launch traced here: 58 us
  Pallas kernels  53.5 us (92%)
  local copies, waits for them, and re-layouts  3.82 us (7%)
  between operations  0.65 us (1%)
    pallas_call x1, Pallas kernels, per_device(): pl.pallas_call(kernel, out_shape=(jax.ShapeDtypeStruct((ATOMS_LOCAL, SUB...  53.5 us
    unnamed x4, local copies, waits for them, and re-layouts  3.82 us

profile of v4, /device:TPU:1, one launch (start us, length us, event | category | flops | bytes accessed | tf_op | source)
XLA Modules:
  0.0 58.0 jit_solution(15757841807295088462)
XLA Ops:
  0.6 53.5 %superpose.1 = (f32[384,1536]{1,0:T(8,128)}, f32[3,3,32]{2,1,0:T(4,128)}) custom-call(bf16[96,384]{1,0:T(8,128)(2,1)} %bitcast.3, f32[3,3,256]{2,1,0:T(4,128)} %rot_hbm.1, f32[384,1536]{1,0:T(8,128)} %w_hbm.1), custom_call_target="tpu_custom_call" | custom-call | tf_op jit(solution)/shard_map/superpose/pallas_call | solution.py:432
  54.2 0.0 copy-start
  54.2 3.2 %copy.7 = f32[384,1536]{1,0:T(8,128)} copy(f32[384,1536]{1,0:T(8,128)} %get-tuple-element.4) | data formatting | bytes 4718592
  57.4 0.0 copy-done
  57.4 0.6 %copy.8 = f32[3,3,32]{2,1,0:T(4,128)} copy(f32[3,3,32]{2,1,0:T(4,128)S(1)} %copy-done) | data formatting | bytes 2304
Async XLA Ops:
  54.2 3.2 %copy-start = (f32[3,3,32]{2,1,0:T(4,128)S(1)}, f32[3,3,32]{2,1,0:T(4,128)}, u32[]{:S(2)}) copy-start(f32[3,3,32]{2,1,0:T(4,128)} %get-tuple-element.5) | copy-start | bytes 3460

commit v5 on v4

--- a/solution.py
+++ b/solution.py
@@ -61,18 +61,15 @@
 
 
 def kernel(
-    x_hbm, rot_hbm, w_hbm, cov_hbm, tr_ref,
-    rot, wv, cpart, cbuf, csum, hsend, hbuf, asend, abuf, bsend, bbuf, turn, rbuf, ybuf, pbuf, acc, coef, wide, dev_rows, dev_q, out,
-    in_sem, out_sem, c_send, c_recv, h_send, h_recv, a_send, a_recv, b_send, b_recv, r_send, r_recv, z_send, z_recv,
+    x_hbm, rot_hbm, w_hbm, dev_rows, dev_cols, tr_ref,
+    rot, wv, cpart, cbuf, csend, cring, csum, hsend, hbuf, asend, abuf, bsend, bbuf, turn, rbuf, ybuf, pbuf, acc, coef, wide, dev_q,
+    in_sem, c_send, c_recv, d_send, d_recv, h_send, h_recv, a_send, a_recv, b_send, b_recv, r_send, r_recv, z_send, z_recv,
     y_send, y_recv, x_send, x_recv, s_send, s_recv,
 ):
     row = lax.axis_index("row")
     col = lax.axis_index("col")
     core = row % 2
     sibling = row + 1 - 2 * core
-    panel_col = row // SUB
-    sub = row % SUB
-    is_self = panel_col == col
     y, zl = row // 8, lax.rem(row // 2, 4)
     x, zh = col // 2, lax.rem(col, 2)
     half = zl // 2
@@ -102,14 +99,6 @@
 
     def greet(r, c):
         pl.semaphore_signal(barrier, inc=1, device_id=(r, c), device_id_type=MESH)
-
-    for m in range(16):
-        r = SUB * col + 2 * (m // COLS) + core
-        c = m % COLS
-
-        @pl.when(jnp.logical_or(r != row, c != col))
-        def _():
-            greet(r, c)
 
     for m in range(1, 16):
         greet(*plane_peer(m))
@@ -131,15 +120,15 @@
     for l in range(3):
         cpart[0:1, l * ATOMS_LOCAL : (l + 1) * ATOMS_LOCAL] = part[l : l + 1, :]
 
-    @pl.when(is_self)
+    @pl.when(x == y)
     def _():
-        cbuf[sub // 2, col] = cpart[...]
+        cbuf[x] = cpart[...]
 
     @pl.when(in_half)
     def _():
         ybuf[y, 2 * (zl % 2) + zh] = x_ref[...]
 
-    pl.semaphore_wait(barrier, 39 - is_self.astype(jnp.int32))
+    pl.semaphore_wait(barrier, 23)
 
     def z_copy(i):
         return remote(x_ref, ybuf.at[y, 2 * (zl % 2) + zh], z_send.at[i], z_recv.at[zl % 2, zh], *dev(x, y, half, zl + i))
@@ -163,17 +152,38 @@
         return remote(pbuf.at[core, k], pbuf.at[core, k], s_send.at[k], s_recv.at[k], sibling, col)
 
     def chunk(n):
-        return 2 * (n % 2) + (zh if n < 2 else 1 - zh)
+        odd = lax.rem(zl, 2)
+        near = jnp.where(in_half, odd, 1 - odd)
+        turn_at = (True, False, in_half, jnp.logical_not(in_half))[n]
+        j = near if n == 0 else 1 - near if n == 1 else jnp.where(turn_at, near, 1 - near)
+        h = jnp.where(in_half, zh, odd)
+        return 2 * j + (h if n < 2 else 1 - h)
 
     def y_step(n):
         k = chunk(n)
 
-        @pl.when(jnp.logical_or(jnp.logical_not(in_half), zl % 2 != n % 2))
-        def _():
-            remote(x_ref, ybuf.at[y, k], z_send.at[0], z_recv.at[k // 2, k % 2], row, col).wait_recv()
-
-        for i in range(1, 4):
-            y_copy(i, k).start()
+        def forward():
+            for i in range(1, 4):
+                y_copy(i, k).start()
+
+        def await_z():
+            remote(x_ref, ybuf.at[y, k], z_send.at[0], z_recv.at[k // 2, lax.rem(k, 2)], row, col).wait_recv()
+
+        if n % 2:
+            await_z()
+            forward()
+        else:
+
+            @pl.when(jnp.logical_not(in_half))
+            def _():
+                await_z()
+                forward()
+
+            if n:
+
+                @pl.when(in_half)
+                def _():
+                    forward()
 
     def x_step(n):
         k = chunk(n)
@@ -199,24 +209,52 @@
             remote(x_ref, pbuf.at[core, k, there], x_send.at[0, 0], x_recv.at[k, there], row, col).wait_recv()
         share_copy(k).start()
 
+    def centre_copy(i):
+        return remote(cpart, cbuf.at[x], c_send.at[i], c_recv.at[x], *dev(y, y + i, zh, zl))
+
+    def ring_part_copy(i):
+        slot = 2 * lax.rem(zl, 2) + zh
+        return remote(csend, cring.at[slot], d_send.at[i], d_recv.at[slot], *dev(x, y, half, zl + i))
+
+    for i in range(4):
+        if i:
+            centre_copy(i).start()
+        else:
+
+            @pl.when(x != y)
+            def _():
+                centre_copy(0).start()
+
     pair_copy().start()
     for i in range(1, 4):
         z_copy(i).start()
     for i in range(1, 4):
         row_copy(i, False).start()
 
-    def centre_copy(m):
-        r = 2 * lax.rem(row // 2 + m, 16) + core
-        return remote(cpart, cbuf.at[sub // 2, col], c_send.at[m], c_recv.at[sub // 2, col], r, panel_col)
-
-    for m in range(16):
-        if m:
-            centre_copy(m).start()
+    @pl.when(in_half)
+    def _():
+        for i in range(1, 4):
+            y_copy(i, 2 * (zl % 2) + zh).start()
+
+    for p in range(4):
+
+        @pl.when(jnp.logical_or(p != x, x != y))
+        def _():
+            remote(cpart, cbuf.at[p], c_send.at[0], c_recv.at[p], row, col).wait_recv()
+
+    csend[...] = (cbuf[0] + cbuf[1]) + (cbuf[2] + cbuf[3])
+    for i in range(4):
+        if i:
+            ring_part_copy(i).start()
         else:
 
-            @pl.when(jnp.logical_not(is_self))
-            def _():
-                centre_copy(0).start()
+            @pl.when(jnp.logical_not(in_half))
+            def _():
+                ring_part_copy(0).start()
+
+    @pl.when(in_half)
+    def _():
+        cring[2 * lax.rem(zl, 2) + zh] = csend[...]
 
     other_slot = 2 * x + 1 - zh
     remote(x_ref, rbuf.at[other_slot], z_send.at[0], r_recv.at[other_slot], row, col).wait_recv()
@@ -227,25 +265,24 @@
     def _():
         ybuf[y, 2 * (zl % 2) + 1 - zh] = rbuf[other_slot]
 
+
     y_step(0)
     y_step(1)
-
+    y_step(2)
     for j in range(2):
-        for c in range(COLS):
-
-            @pl.when(jnp.logical_or(SUB * col + 2 * j + core != row, c != col))
-            def _():
-                remote(cpart, cbuf.at[j, c], c_send.at[0], c_recv.at[j, c], row, col).wait_recv()
-
-    csum[core] = jnp.sum(cbuf[...], axis=1) * (1.0 / FRAMES)
+        for h in range(2):
+
+            @pl.when(jnp.logical_or(jnp.logical_not(in_half), jnp.logical_or(lax.rem(zl, 2) != j, zh != h)))
+            def _():
+                remote(csend, cring.at[2 * j + h], d_send.at[0], d_recv.at[2 * j + h], row, col).wait_recv()
+
+        csum[core, j] = (cring[2 * j] + cring[2 * j + 1]) * (1.0 / FRAMES)
 
     def half_copy(i, src, dst):
         return remote(src, dst, h_send.at[i], h_recv.at[i], sibling, col)
 
     centre_half = half_copy(0, csum.at[core], csum.at[core])
     centre_half.start()
-    y_step(2)
-    y_step(3)
     half_copy(0, csum.at[core], csum.at[1 - core]).wait_recv()
 
     w_load.wait()
@@ -270,6 +307,7 @@
     chooser = jnp.where(owner_of == lax.broadcasted_iota(jnp.int32, shape, 0), 1.0, 0.0).astype(BF16)
     weighted = contract(chooser, acc[...], ((1,), (1,)))
 
+    y_step(3)
     for i in range(1, 4):
         for h in range(2):
             slot = 2 * lax.rem(x + i, 4) + h
@@ -303,6 +341,7 @@
     for m in range(1, 16):
         plane_copy(m).start()
     x_step(1)
+    x_step(2)
     for m in range(1, 16):
         slot = 4 * lax.rem(x + m // 4, 4) + lax.rem(y + m % 4, 4)
         remote(asend, abuf.at[slot], a_send.at[0], a_recv.at[slot], row, col).wait_recv()
@@ -310,11 +349,10 @@
     bbuf[z] = bsend[...]
     for m in range(1, 8):
         ring_copy(m).start()
-    x_step(2)
+
     x_step(3)
     share_step(0)
     share_step(1)
-
     centre_rows = jnp.zeros((8, ATOMS_LOCAL), F32)
     for l in range(3):
         frames_l = rbuf[:, l * FB : (l + 1) * FB, :].reshape(FRAMES, ATOMS_LOCAL)
@@ -353,13 +391,13 @@
             for j in range(9):
                 wide[j, 4 * half_of + c] = jnp.broadcast_to(upright[c * FB : (c + 1) * FB, j : j + 1], (FB, 128))
 
-    def deviate(block_of, centre):
+    def deviate(target, count, block_of, start_of, centre):
         base = [jnp.broadcast_to(centre[k], (FB, ATOMS_LOCAL)) for k in range(3)]
 
-        def body(c, carry):
-            block = block_of(c).astype(F32)
+        def body(i, carry):
+            block = block_of(i).astype(F32)
             xs = [block[l * FB : (l + 1) * FB, :] for l in range(3)]
-            start = pl.multiple_of(c * 96, 96)
+            c = start_of(i)
             values = []
             for k in range(3):
                 terms = []
@@ -367,43 +405,48 @@
                     factor = wide[3 * k + l, c]
                     terms.append(jnp.concatenate([factor, factor, factor], axis=1) * xs[l])
                 values.append((terms[0] + terms[1]) + terms[2] - base[k])
-            dev_q[pl.ds(start, 96), :] = jnp.concatenate(values, axis=0).astype(BF16)
+            target[pl.ds(pl.multiple_of(c * 96, 96), 96), :] = jnp.concatenate(values, axis=0).astype(BF16)
             return carry
 
-        lax.fori_loop(0, COLS, body, 0)
-
-    deviate(lambda c: rbuf[c], [centre_rows[k : k + 1, :] for k in range(3)])
+        lax.fori_loop(0, count, body, 0)
+
+    def deviate_piece(owner, n):
+        k = chunk(n)
+        j = k // 2
+        centre = [csum[owner, j, :, i * ATOMS_LOCAL : (i + 1) * ATOMS_LOCAL] for i in range(3)]
+        deviate(
+            dev_cols.at[2 * j + owner], 4, lambda i: pbuf[owner, k, i], lambda i: 2 * i + lax.rem(k, 2), centre
+        )
+
+    def shared_wait(n):
+        k = chunk(n)
+        remote(pbuf.at[1 - core, k], pbuf.at[1 - core, k], s_send.at[0], s_recv.at[k], row, col).wait_recv()
+
+    deviate(dev_q, COLS, lambda i: rbuf[i], lambda i: i, [centre_rows[k : k + 1, :] for k in range(3)])
     dev_rows[...] = jnp.transpose(dev_q[...])
     share_step(3)
-
-    def out_copy(q):
-        start = pl.multiple_of(q * ATOMS_LOCAL, ATOMS_LOCAL)
-        return pltpu.make_async_copy(out.at[q], cov_hbm.at[:, pl.ds(start, ATOMS_LOCAL)], out_sem.at[q])
-
-    for side in range(2):
-        owner = core if side == 0 else 1 - core
-        for j in range(2):
-            if side:
-                for h in range(2):
-                    k = 2 * j + h
-                    remote(pbuf.at[owner, k], pbuf.at[owner, k], s_send.at[0], s_recv.at[k], row, col).wait_recv()
-            q = 2 * j + owner
-            centre_q = [csum[owner, j, :, k * ATOMS_LOCAL : (k + 1) * ATOMS_LOCAL] for k in range(3)]
-            deviate(lambda c: pbuf[owner, 2 * j + lax.rem(c, 2), c // 2], centre_q)
-            out[q] = contract(dev_rows[...], dev_q[...], ((1,), (0,))) * (1.0 / (3 * FRAMES))
-            out_copy(q).start()
-
-    for q in range(SUB):
-        out_copy(q).wait()
-
-    for m in range(16):
-        if m:
-            centre_copy(m).wait_send()
+    for n in range(3):
+        deviate_piece(core, n)
+    for n in range(3):
+        shared_wait(n)
+        deviate_piece(1 - core, n)
+    deviate_piece(core, 3)
+    shared_wait(3)
+    deviate_piece(1 - core, 3)
+
+    for i in range(4):
+        if i:
+            centre_copy(i).wait_send()
+            ring_part_copy(i).wait_send()
         else:
 
-            @pl.when(jnp.logical_not(is_self))
+            @pl.when(x != y)
             def _():
                 centre_copy(0).wait_send()
+
+            @pl.when(jnp.logical_not(in_half))
+            def _():
+                ring_part_copy(0).wait_send()
 
     for m in range(1, 16):
         plane_copy(m).wait_send()
@@ -424,24 +467,34 @@
         share_copy(k).wait_send()
 
 
+def multiply(rows_ref, cols_ref, tr_ref, cov_ref, out_ref):
+    q = pl.program_id(0)
+    out_ref[...] = tr_ref[...]
+    cov_ref[...] = contract(rows_ref[...], cols_ref[q], ((1,), (0,))) * (1.0 / (3 * FRAMES))
+
+
 def per_device(frames, rotations, inverse_cov):
     x = jnp.transpose(frames, (1, 0, 2)).reshape(96, ATOMS_LOCAL)
     dma = pltpu.SemaphoreType.DMA
     vmem = pl.BlockSpec(memory_space=pltpu.VMEM)
     hbm = pl.BlockSpec(memory_space=pltpu.HBM)
-    return pl.pallas_call(
+    operands = [pltpu.with_memory_space_constraint(value, pltpu.HBM) for value in (x, rotations, inverse_cov)]
+    dev_rows, dev_cols, turned = pl.pallas_call(
         kernel,
         out_shape=(
-            jax.ShapeDtypeStruct((ATOMS_LOCAL, SUB * ATOMS_LOCAL), F32),
+            jax.ShapeDtypeStruct((ATOMS_LOCAL, 3 * FRAMES), BF16),
+            jax.ShapeDtypeStruct((SUB, 3 * FRAMES, ATOMS_LOCAL), BF16),
             jax.ShapeDtypeStruct((3, 3, FB), F32),
         ),
         in_specs=[hbm, hbm, hbm],
-        out_specs=(pl.BlockSpec(memory_space=pl.ANY), vmem),
+        out_specs=(vmem, vmem, vmem),
         scratch_shapes=[
             pltpu.VMEM((3, 3, 256), F32),
             pltpu.VMEM((384, 1536), F32),
             pltpu.VMEM((1, 1152), F32),
-            pltpu.VMEM((2, 8, 1, 1152), F32),
+            pltpu.VMEM((4, 1, 1152), F32),
+            pltpu.VMEM((1, 1152), F32),
+            pltpu.VMEM((4, 1, 1152), F32),
             pltpu.VMEM((2, 2, 1, 1152), F32),
             pltpu.VMEM((1, 1152), F32),
             pltpu.VMEM((1, 1, 1152), F32),
@@ -456,11 +509,10 @@
             pltpu.VMEM((384, 1152), BF16),
             pltpu.VMEM((16, 128), F32),
             pltpu.VMEM((9, 8, 32, 128), F32),
-            pltpu.VMEM((384, 768), BF16),
             pltpu.VMEM((768, 384), BF16),
-            pltpu.VMEM((4, 384, 384), F32),
-            dma((3,)), dma((4,)),
-            dma((16,)), dma((2, 8)),
+            dma((3,)),
+            dma((4,)), dma((4,)),
+            dma((4,)), dma((4,)),
             dma((3,)), dma((3,)),
             dma((16,)), dma((16,)),
             dma((8,)), dma((8,)),
@@ -471,10 +523,27 @@
             dma((4,)), dma((4,)),
         ],
         compiler_params=pltpu.CompilerParams(
-            collective_id=0, has_side_effects=True, vmem_limit_bytes=56 * 1024 * 1024
+            collective_id=0, has_side_effects=True, vmem_limit_bytes=32 * 1024 * 1024
         ),
         name="superpose",
-    )(x, rotations, inverse_cov)
+    )(*operands)
+    return pl.pallas_call(
+        multiply,
+        grid=(SUB,),
+        out_shape=(
+            jax.ShapeDtypeStruct((ATOMS_LOCAL, SUB * ATOMS_LOCAL), F32),
+            jax.ShapeDtypeStruct((3, 3, FB), F32),
+        ),
+        in_specs=[vmem, vmem, vmem],
+        out_specs=(
+            pl.BlockSpec((ATOMS_LOCAL, ATOMS_LOCAL), lambda q: (0, q)),
+            pl.BlockSpec((3, 3, FB), lambda q: (0, 0, 0)),
+        ),
+        compiler_params=pltpu.CompilerParams(
+            dimension_semantics=("arbitrary",), vmem_limit_bytes=16 * 1024 * 1024
+        ),
+        name="covariance",
+    )(dev_rows, dev_cols, turned)
 
 
 def solution(mesh):

time: 58.2 us -> 52.7 us (0.905)
  local copies, waits for them, and re-layouts: 3.82 us -> 0 us
  Pallas kernels: 53.5 us -> 52 us
    unnamed x4 -> x0, local copies, waits for them, and re-layouts: 3.82 us -> none
    pallas_call x1 -> x2, Pallas kernels: 53.5 us -> 52 us  [the longest x1 48.9 us: per_device(): pl.pallas_call(kernel, out_shape=(jax.ShapeDtypeStruct((ATOMS_LOCAL, 3 *...]
where the time goes in v5:
time: 52.7 us; the launch traced here: 52.6 us
  Pallas kernels  52 us (99%)
  between operations  0.64 us (1%)
    pallas_call x1, Pallas kernels, per_device(): pl.pallas_call(kernel, out_shape=(jax.ShapeDtypeStruct((ATOMS_LOCAL, 3 *...  48.9 us
    pallas_call x1, Pallas kernels, per_device(): pl.pallas_call(multiply, grid=(SUB,), out_shape=(jax.ShapeDtypeStruct((AT...  3.08 us

profile of v5, /device:TPU:1, one launch (start us, length us, event | category | flops | bytes accessed | tf_op | source)
XLA Modules:
  0.0 52.6 jit_solution(1390932158414740950)
XLA Ops:
  0.6 48.9 %superpose.1 = (bf16[384,768]{1,0:T(8,128)(2,1)S(1)}, bf16[4,768,384]{2,1,0:T(8,128)(2,1)S(1)}, f32[3,3,32]{2,1,0:T(4,128)S(1)}) custom-call(bf16[96,384]{1,0:T(8,128)(2,1)} %bitcast.3, f32[3,3,256]{2,1,0:T(4,128)} %rot_hbm.1, f32[384,1536]{1,0:T(8,128)} %w_hbm.1), custom_call_target="tpu_custom_call" | custom-call | tf_op jit(solution)/shard_map/superpose/pallas_call | solution.py:482
  49.5 3.1 %covariance.1 = (f32[384,1536]{1,0:T(8,128)}, f32[3,3,32]{2,1,0:T(4,128)}) custom-call(bf16[384,768]{1,0:T(8,128)(2,1)S(1)} %get-tuple-element.5.rows_ref, bf16[4,768,384]{2,1,0:T(8,128)(2,1)S(1)} %get-tuple-element.6.cols_ref, f32[3,3,32]{2,1,0:T(4,128)S(1)} %get-tuple-element.7.tr_ref), custom_call_target="tpu_custom_call" | custom-call | tf_op jit(solution)/shard_map/covariance/pallas_call | solution.py:530

commit v6 on v5

--- a/solution.py
+++ b/solution.py
@@ -64,6 +64,7 @@
     x_hbm, rot_hbm, w_hbm, dev_rows, dev_cols, tr_ref,
     rot, wv, cpart, cbuf, csend, cring, csum, hsend, hbuf, asend, abuf, bsend, bbuf, turn, rbuf, ybuf, pbuf, acc, coef, wide, dev_q,
     in_sem, c_send, c_recv, d_send, d_recv, h_send, h_recv, a_send, a_recv, b_send, b_recv, r_send, r_recv, z_send, z_recv,
+    pair_send,
     y_send, y_recv, x_send, x_recv, s_send, s_recv,
 ):
     row = lax.axis_index("row")
@@ -130,11 +131,31 @@
 
     pl.semaphore_wait(barrier, 23)
 
-    def z_copy(i):
-        return remote(x_ref, ybuf.at[y, 2 * (zl % 2) + zh], z_send.at[i], z_recv.at[zl % 2, zh], *dev(x, y, half, zl + i))
+    def any_of(*places):
+        found = z == places[0]
+        for value in places[1:]:
+            found = jnp.logical_or(found, z == value)
+        return found
+
+    steps = ((1, any_of(0, 1, 3, 6)), (-1, any_of(1, 4, 6, 7)), (2, any_of(1, 3)), (-2, any_of(4, 6)))
+
+    def z_copy(m, other):
+        there = lax.rem(z + 8 + steps[m][0], 8)
+        h = 1 - zh if other else zh
+        return remote(
+            rbuf.at[2 * x + h], ybuf.at[y, 2 * lax.rem(zl, 2) + h], z_send.at[m, int(other)],
+            z_recv.at[lax.rem(zl, 2), h], *dev(x, y, there // 4, there),
+        )
+
+    def for_z(other, action):
+        for m in range(4):
+
+            @pl.when(steps[m][1])
+            def _():
+                action(z_copy(m, other))
 
     def pair_copy():
-        return remote(x_ref, rbuf.at[col], z_send.at[0], r_recv.at[col], *dev(x, y, 1 - zh, zl))
+        return remote(x_ref, rbuf.at[col], pair_send, r_recv.at[col], *dev(x, y, 1 - zh, zl))
 
     def row_copy(i, other):
         slot = 2 * x + (1 - zh if other else zh)
@@ -153,11 +174,9 @@
 
     def chunk(n):
         odd = lax.rem(zl, 2)
-        near = jnp.where(in_half, odd, 1 - odd)
-        turn_at = (True, False, in_half, jnp.logical_not(in_half))[n]
-        j = near if n == 0 else 1 - near if n == 1 else jnp.where(turn_at, near, 1 - near)
-        h = jnp.where(in_half, zh, odd)
-        return 2 * j + (h if n < 2 else 1 - h)
+        j = odd if n % 2 == 0 else 1 - odd
+        h = zh if n < 2 else 1 - zh
+        return jnp.where(in_half, 2 * j + h, (2, 1, 3, 0)[n])
 
     def y_step(n):
         k = chunk(n)
@@ -167,7 +186,7 @@
                 y_copy(i, k).start()
 
         def await_z():
-            remote(x_ref, ybuf.at[y, k], z_send.at[0], z_recv.at[k // 2, lax.rem(k, 2)], row, col).wait_recv()
+            remote(x_ref, ybuf.at[y, k], pair_send, z_recv.at[k // 2, lax.rem(k, 2)], row, col).wait_recv()
 
         if n % 2:
             await_z()
@@ -226,8 +245,7 @@
                 centre_copy(0).start()
 
     pair_copy().start()
-    for i in range(1, 4):
-        z_copy(i).start()
+    for_z(False, lambda copy: copy.start())
     for i in range(1, 4):
         row_copy(i, False).start()
 
@@ -257,7 +275,8 @@
         cring[2 * lax.rem(zl, 2) + zh] = csend[...]
 
     other_slot = 2 * x + 1 - zh
-    remote(x_ref, rbuf.at[other_slot], z_send.at[0], r_recv.at[other_slot], row, col).wait_recv()
+    remote(x_ref, rbuf.at[other_slot], pair_send, r_recv.at[other_slot], row, col).wait_recv()
+    for_z(True, lambda copy: copy.start())
     for i in range(1, 4):
         row_copy(i, True).start()
 
@@ -285,6 +304,7 @@
     centre_half.start()
     half_copy(0, csum.at[core], csum.at[1 - core]).wait_recv()
 
+    x_step(0)
     w_load.wait()
     lanes = [[csum[q % 2, q // 2, :, l * ATOMS_LOCAL : (l + 1) * ATOMS_LOCAL] for q in range(SUB)] for l in range(3)]
 
@@ -307,7 +327,6 @@
     chooser = jnp.where(owner_of == lax.broadcasted_iota(jnp.int32, shape, 0), 1.0, 0.0).astype(BF16)
     weighted = contract(chooser, acc[...], ((1,), (1,)))
 
-    y_step(3)
     for i in range(1, 4):
         for h in range(2):
             slot = 2 * lax.rem(x + i, 4) + h
@@ -326,7 +345,6 @@
             hsend[0:1, at : at + 128] = others[l : l + 1, :]
     fit_half = half_copy(1, hsend, hbuf.at[0])
     fit_half.start()
-    x_step(0)
     fit_half.wait_recv()
     asend[...] = asend[...] + hbuf[0]
     a_slot = 4 * x + y
@@ -340,6 +358,7 @@
 
     for m in range(1, 16):
         plane_copy(m).start()
+    y_step(3)
     x_step(1)
     x_step(2)
     for m in range(1, 16):
@@ -456,8 +475,9 @@
     fit_half.wait_send()
     turn_half.wait_send()
     pair_copy().wait_send()
+    for_z(False, lambda copy: copy.wait_send())
+    for_z(True, lambda copy: copy.wait_send())
     for i in range(1, 4):
-        z_copy(i).wait_send()
         row_copy(i, False).wait_send()
         row_copy(i, True).wait_send()
         for k in range(4):
@@ -517,7 +537,7 @@
             dma((16,)), dma((16,)),
             dma((8,)), dma((8,)),
             dma((2, 4)), dma((8,)),
-            dma((4,)), dma((2, 2)),
+            dma((4, 2)), dma((2, 2)), dma(()),
             dma((4, 4)), dma((4, 4)),
             dma((4, 4)), dma((4, 4)),
             dma((4,)), dma((4,)),

time: 52.7 us -> 47.3 us (0.90)
  Pallas kernels: 52 us -> 46.5 us
    pallas_call x1, Pallas kernels: 48.9 us -> 43.5 us  [per_device(): pl.pallas_call(kernel, out_shape=(jax.ShapeDtypeStruct((ATOMS_LOCAL, 3 *...]
where the time goes in v6:
time: 47.3 us; the launch traced here: 47.2 us
  Pallas kernels  46.5 us (98%)
  between operations  0.64 us (1%)
    pallas_call x1, Pallas kernels, per_device(): pl.pallas_call(kernel, out_shape=(jax.ShapeDtypeStruct((ATOMS_LOCAL, 3 *...  43.5 us
    pallas_call x1, Pallas kernels, per_device(): pl.pallas_call(multiply, grid=(SUB,), out_shape=(jax.ShapeDtypeStruct((AT...  3.08 us

profile of v6, /device:TPU:1, one launch (start us, length us, event | category | flops | bytes accessed | tf_op | source)
XLA Modules:
  0.0 47.2 jit_solution(12847990383852276136)
XLA Ops:
  0.6 43.5 %superpose.1 = (bf16[384,768]{1,0:T(8,128)(2,1)S(1)}, bf16[4,768,384]{2,1,0:T(8,128)(2,1)S(1)}, f32[3,3,32]{2,1,0:T(4,128)S(1)}) custom-call(bf16[96,384]{1,0:T(8,128)(2,1)} %bitcast.3, f32[3,3,256]{2,1,0:T(4,128)} %rot_hbm.1, f32[384,1536]{1,0:T(8,128)} %w_hbm.1), custom_call_target="tpu_custom_call" | custom-call | tf_op jit(solution)/shard_map/superpose/pallas_call | solution.py:502
  44.1 3.1 %covariance.1 = (f32[384,1536]{1,0:T(8,128)}, f32[3,3,32]{2,1,0:T(4,128)}) custom-call(bf16[384,768]{1,0:T(8,128)(2,1)S(1)} %get-tuple-element.5.rows_ref, bf16[4,768,384]{2,1,0:T(8,128)(2,1)S(1)} %get-tuple-element.6.cols_ref, f32[3,3,32]{2,1,0:T(4,128)S(1)} %get-tuple-element.7.tr_ref), custom_call_target="tpu_custom_call" | custom-call | tf_op jit(solution)/shard_map/covariance/pallas_call | solution.py:550

commit v7 on v6

--- a/solution.py
+++ b/solution.py
@@ -178,31 +178,23 @@
         h = zh if n < 2 else 1 - zh
         return jnp.where(in_half, 2 * j + h, (2, 1, 3, 0)[n])
 
+    def y_forward(k):
+        for i in range(1, 4):
+            y_copy(i, k).start()
+
+    def y_arrived(n):
+        k = chunk(n)
+        remote(x_ref, ybuf.at[y, k], pair_send, z_recv.at[k // 2, lax.rem(k, 2)], row, col).wait_recv()
+        y_forward(k)
+
     def y_step(n):
-        k = chunk(n)
-
-        def forward():
-            for i in range(1, 4):
-                y_copy(i, k).start()
-
-        def await_z():
-            remote(x_ref, ybuf.at[y, k], pair_send, z_recv.at[k // 2, lax.rem(k, 2)], row, col).wait_recv()
-
         if n % 2:
-            await_z()
-            forward()
+            y_arrived(n)
         else:
-
-            @pl.when(jnp.logical_not(in_half))
-            def _():
-                await_z()
-                forward()
-
-            if n:
-
-                @pl.when(in_half)
-                def _():
-                    forward()
+            pl.when(jnp.logical_not(in_half))(lambda: y_arrived(n))
+
+    def y_held():
+        pl.when(in_half)(lambda: y_forward(chunk(2)))
 
     def x_step(n):
         k = chunk(n)
@@ -287,7 +279,7 @@
 
     y_step(0)
     y_step(1)
-    y_step(2)
+    y_held()
     for j in range(2):
         for h in range(2):
 
@@ -304,7 +296,6 @@
     centre_half.start()
     half_copy(0, csum.at[core], csum.at[1 - core]).wait_recv()
 
-    x_step(0)
     w_load.wait()
     lanes = [[csum[q % 2, q // 2, :, l * ATOMS_LOCAL : (l + 1) * ATOMS_LOCAL] for q in range(SUB)] for l in range(3)]
 
@@ -358,7 +349,9 @@
 
     for m in range(1, 16):
         plane_copy(m).start()
+    y_step(2)
     y_step(3)
+    x_step(0)
     x_step(1)
     x_step(2)
     for m in range(1, 16):
@@ -369,9 +362,9 @@
     for m in range(1, 8):
         ring_copy(m).start()
 
-    x_step(3)
     share_step(0)
     share_step(1)
+    x_step(3)
     centre_rows = jnp.zeros((8, ATOMS_LOCAL), F32)
     for l in range(3):
         frames_l = rbuf[:, l * FB : (l + 1) * FB, :].reshape(FRAMES, ATOMS_LOCAL)
@@ -379,6 +372,33 @@
         product = contract(jnp.concatenate(split3(spin), axis=0), frames_l, ((1,), (0,)))
         centre_rows = centre_rows + (product[0:8] + product[8:16] + product[16:24])
     centre_rows = centre_rows * (1.0 / FRAMES)
+
+    for i in range(4):
+        if i:
+            centre_copy(i).wait_send()
+            ring_part_copy(i).wait_send()
+        else:
+
+            @pl.when(x != y)
+            def _():
+                centre_copy(0).wait_send()
+
+            @pl.when(jnp.logical_not(in_half))
+            def _():
+                ring_part_copy(0).wait_send()
+
+    for m in range(1, 16):
+        plane_copy(m).wait_send()
+    centre_half.wait_send()
+    fit_half.wait_send()
+    pair_copy().wait_send()
+    for_z(False, lambda copy: copy.wait_send())
+    for_z(True, lambda copy: copy.wait_send())
+    for i in range(1, 4):
+        row_copy(i, False).wait_send()
+        row_copy(i, True).wait_send()
+        for n in range(3):
+            y_copy(i, chunk(n)).wait_send()
 
     for m in range(1, 8):
         slot = lax.rem(z + m, 8)
@@ -453,44 +473,29 @@
     shared_wait(3)
     deviate_piece(1 - core, 3)
 
-    for i in range(4):
-        if i:
-            centre_copy(i).wait_send()
-            ring_part_copy(i).wait_send()
-        else:
-
-            @pl.when(x != y)
-            def _():
-                centre_copy(0).wait_send()
-
-            @pl.when(jnp.logical_not(in_half))
-            def _():
-                ring_part_copy(0).wait_send()
-
-    for m in range(1, 16):
-        plane_copy(m).wait_send()
     for m in range(1, 8):
         ring_copy(m).wait_send()
-    centre_half.wait_send()
-    fit_half.wait_send()
     turn_half.wait_send()
-    pair_copy().wait_send()
-    for_z(False, lambda copy: copy.wait_send())
-    for_z(True, lambda copy: copy.wait_send())
+    for n in range(4):
+        for i in range(1, 4):
+            x_copy(i, chunk(n)).wait_send()
+        share_copy(chunk(n)).wait_send()
     for i in range(1, 4):
-        row_copy(i, False).wait_send()
-        row_copy(i, True).wait_send()
-        for k in range(4):
-            y_copy(i, k).wait_send()
-            x_copy(i, k).wait_send()
-    for k in range(4):
-        share_copy(k).wait_send()
-
-
-def multiply(rows_ref, cols_ref, tr_ref, cov_ref, out_ref):
-    q = pl.program_id(0)
-    out_ref[...] = tr_ref[...]
-    cov_ref[...] = contract(rows_ref[...], cols_ref[q], ((1,), (0,))) * (1.0 / (3 * FRAMES))
+        y_copy(i, chunk(3)).wait_send()
+
+
+def multiply(rows_ref, cols_ref, tr_ref, cov_hbm, out_hbm, block, sem):
+    out_copy = pltpu.make_async_copy(tr_ref, out_hbm, sem.at[SUB])
+    out_copy.start()
+    copies = []
+    for q in range(SUB):
+        block[q] = contract(rows_ref[...], cols_ref[q], ((1,), (0,))) * (1.0 / (3 * FRAMES))
+        target = cov_hbm.at[:, q * ATOMS_LOCAL : (q + 1) * ATOMS_LOCAL]
+        copies.append(pltpu.make_async_copy(block.at[q], target, sem.at[q]))
+        copies[q].start()
+    for copy in copies:
+        copy.wait()
+    out_copy.wait()
 
 
 def per_device(frames, rotations, inverse_cov):
@@ -549,19 +554,14 @@
     )(*operands)
     return pl.pallas_call(
         multiply,
-        grid=(SUB,),
         out_shape=(
             jax.ShapeDtypeStruct((ATOMS_LOCAL, SUB * ATOMS_LOCAL), F32),
             jax.ShapeDtypeStruct((3, 3, FB), F32),
         ),
         in_specs=[vmem, vmem, vmem],
-        out_specs=(
-            pl.BlockSpec((ATOMS_LOCAL, ATOMS_LOCAL), lambda q: (0, q)),
-            pl.BlockSpec((3, 3, FB), lambda q: (0, 0, 0)),
-        ),
-        compiler_params=pltpu.CompilerParams(
-            dimension_semantics=("arbitrary",), vmem_limit_bytes=16 * 1024 * 1024
-        ),
+        out_specs=(hbm, hbm),
+        scratch_shapes=[pltpu.VMEM((SUB, ATOMS_LOCAL, ATOMS_LOCAL), F32), dma((SUB + 1,))],
+        compiler_params=pltpu.CompilerParams(vmem_limit_bytes=16 * 1024 * 1024),
         name="covariance",
     )(dev_rows, dev_cols, turned)
 

time: 47.3 us -> 45.9 us (0.970)
  Pallas kernels: 46.5 us -> 45.1 us
    pallas_call x1, Pallas kernels: 3.08 us -> 2.25 us  [per_device(): pl.pallas_call(multiply, out_shape=(jax.ShapeDtypeStruct((ATOMS_LOCAL, SU...]
    pallas_call x1, Pallas kernels: 43.5 us -> 42.9 us  [per_device(): pl.pallas_call(kernel, out_shape=(jax.ShapeDtypeStruct((ATOMS_LOCAL, 3 *...]
where the time goes in v7:
time: 45.9 us; the launch traced here: 45.8 us
  Pallas kernels  45.1 us (98%)
  between operations  0.64 us (1%)
    pallas_call x1, Pallas kernels, per_device(): pl.pallas_call(kernel, out_shape=(jax.ShapeDtypeStruct((ATOMS_LOCAL, 3 *...  42.9 us
    pallas_call x1, Pallas kernels, per_device(): pl.pallas_call(multiply, out_shape=(jax.ShapeDtypeStruct((ATOMS_LOCAL, SU...  2.25 us

profile of v7, /device:TPU:1, one launch (start us, length us, event | category | flops | bytes accessed | tf_op | source)
XLA Modules:
  0.0 45.8 jit_solution(7957012029872951699)
XLA Ops:
  0.6 42.9 %superpose.1 = (bf16[384,768]{1,0:T(8,128)(2,1)S(1)}, bf16[4,768,384]{2,1,0:T(8,128)(2,1)S(1)}, f32[3,3,32]{2,1,0:T(4,128)S(1)}) custom-call(bf16[96,384]{1,0:T(8,128)(2,1)} %bitcast.3, f32[3,3,256]{2,1,0:T(4,128)} %rot_hbm.1, f32[384,1536]{1,0:T(8,128)} %w_hbm.1), custom_call_target="tpu_custom_call" | custom-call | tf_op jit(solution)/shard_map/superpose/pallas_call | solution.py:507
  43.5 2.2 %covariance.1 = (f32[384,1536]{1,0:T(8,128)}, f32[3,3,32]{2,1,0:T(4,128)}) custom-call(bf16[384,768]{1,0:T(8,128)(2,1)S(1)} %get-tuple-element.5.rows_ref, bf16[4,768,384]{2,1,0:T(8,128)(2,1)S(1)} %get-tuple-element.6.cols_ref, f32[3,3,32]{2,1,0:T(4,128)S(1)} %get-tuple-element.7.tr_ref), custom_call_target="tpu_custom_call" | custom-call | tf_op jit(solution)/shard_map/covariance/pallas_call | solution.py:555

commit v8 on v7

--- a/solution.py
+++ b/solution.py
@@ -461,14 +461,14 @@
         k = chunk(n)
         remote(pbuf.at[1 - core, k], pbuf.at[1 - core, k], s_send.at[0], s_recv.at[k], row, col).wait_recv()
 
+    share_step(3)
     deviate(dev_q, COLS, lambda i: rbuf[i], lambda i: i, [centre_rows[k : k + 1, :] for k in range(3)])
-    dev_rows[...] = jnp.transpose(dev_q[...])
-    share_step(3)
     for n in range(3):
         deviate_piece(core, n)
     for n in range(3):
         shared_wait(n)
         deviate_piece(1 - core, n)
+    dev_rows[...] = jnp.transpose(dev_q[...])
     deviate_piece(core, 3)
     shared_wait(3)
     deviate_piece(1 - core, 3)

time: 45.9 us -> 45.9 us (level)
  no operation moved by 1% of the time
where the time goes in v8:
time: 45.9 us; the launch traced here: 45.8 us
  Pallas kernels  45.1 us (98%)
  between operations  0.64 us (1%)
    pallas_call x1, Pallas kernels, per_device(): pl.pallas_call(kernel, out_shape=(jax.ShapeDtypeStruct((ATOMS_LOCAL, 3 *...  42.9 us
    pallas_call x1, Pallas kernels, per_device(): pl.pallas_call(multiply, out_shape=(jax.ShapeDtypeStruct((ATOMS_LOCAL, SU...  2.25 us

profile of v8, /device:TPU:1, one launch (start us, length us, event | category | flops | bytes accessed | tf_op | source)
XLA Modules:
  0.0 45.8 jit_solution(4352843722542647580)
XLA Ops:
  0.6 42.9 %superpose.1 = (bf16[384,768]{1,0:T(8,128)(2,1)S(1)}, bf16[4,768,384]{2,1,0:T(8,128)(2,1)S(1)}, f32[3,3,32]{2,1,0:T(4,128)S(1)}) custom-call(bf16[96,384]{1,0:T(8,128)(2,1)} %bitcast.3, f32[3,3,256]{2,1,0:T(4,128)} %rot_hbm.1, f32[384,1536]{1,0:T(8,128)} %w_hbm.1), custom_call_target="tpu_custom_call" | custom-call | tf_op jit(solution)/shard_map/superpose/pallas_call | solution.py:507
  43.5 2.2 %covariance.1 = (f32[384,1536]{1,0:T(8,128)}, f32[3,3,32]{2,1,0:T(4,128)}) custom-call(bf16[384,768]{1,0:T(8,128)(2,1)S(1)} %get-tuple-element.5.rows_ref, bf16[4,768,384]{2,1,0:T(8,128)(2,1)S(1)} %get-tuple-element.6.cols_ref, f32[3,3,32]{2,1,0:T(4,128)S(1)} %get-tuple-element.7.tr_ref), custom_call_target="tpu_custom_call" | custom-call | tf_op jit(solution)/shard_map/covariance/pallas_call | solution.py:555
